TPU v7x, 1024 devices: a whole 4x4x32 slice. The times are simulated.
1024 devices in a mesh: seq: 32 (over y, z_lo), head: 32 (over x, z_hi, core).
Axes of the slice: x: 4, y: 4, z: 32 (z_hi: 4, z_lo: 8; z = z_hi * 8 + z_lo), core: 2. Of those that a mesh axis runs over, the one named last changes fastest.
Arguments:
- query_heads: bfloat16 [16384, 4096], P('seq', 'head'), may hold values from -5 to 5
- key_heads: bfloat16 [16384, 4096], P('seq', 'head'), may hold values from -5 to 5
- value_heads: bfloat16 [16384, 4096], P('seq', 'head'), may hold values from -6 to 6
- grad_out: bfloat16 [16384, 4096], P(('seq', 'head')), may hold values from -6 to 6
- saved_out: bfloat16 [16384, 4096], P(('seq', 'head')), may hold values from -6 to 6
- block_list: int32 [128, 8], replicated, may hold values from -1 to 7, as said below
Outputs:
- grad_query: bfloat16 [16384, 4096], P(('seq', 'head'))
- grad_key: bfloat16 [16384, 4096], P(('seq', 'head'))
- grad_value: bfloat16 [16384, 4096], P(('seq', 'head'))
Inputs may be any that keep to these rules, and one draw needn't show every extreme that they name: `block_list`: row b lists first its own diagonal block 4 + b % 4, then distinct earlier blocks of its own group or blocks of the preceding group (none for the first group), then -1 for the remaining entries; the last query block of the sequence lists 8 blocks.
All inputs are finite; a program needn't handle non-finite values.
Results may differ from a plain program's by a relative error of at most 0.0065.
Values may be sent and summed in bfloat16 or wider, within the bound.
No kernel may reach another device: no remote copies, remote signals or barrier semaphores. Data moves between devices by JAX's collectives and lax.ppermute only.
A program may use at most 32 MiB of HBM per device.

v0:
```python
import jax
import jax.numpy as jnp
from jax import lax
from jax.sharding import PartitionSpec as P

HD = 128
BLK = 128
MAXSEL = 8


def shifted(value, axis, by):
    size = lax.axis_size(axis)
    pairs = [(i, i + by) for i in range(size) if 0 <= i + by < size]
    return lax.ppermute(value, axis, pairs)


def block_scores(query_blocks, key_blocks, block_index, key_limit):
    qcount = query_blocks.shape[0]
    picked = jnp.maximum(block_index, 0)
    key_tiles = key_blocks[picked]
    scores = jnp.einsum(
        "qid,qjd->qij", query_blocks, key_tiles, preferred_element_type=jnp.float32
    ) * HD ** (-0.5)
    diagonal = block_index == qcount + jnp.arange(qcount, dtype=jnp.int32)
    lower_mask = (
        jnp.arange(BLK, dtype=jnp.int32)[:, None] >= jnp.arange(BLK, dtype=jnp.int32)[None, :]
    )
    allowed = ((block_index >= 0) & (block_index < key_limit))[:, None, None] & (
        (~diagonal)[:, None, None] | lower_mask[None]
    )
    return (picked, key_tiles, scores, allowed)


def log_totals(query_blocks, key_blocks, block_rows):
    qcount = query_blocks.shape[0]
    running_max = jnp.full((qcount, BLK), -1e30, jnp.float32)
    running_sum = jnp.zeros((qcount, BLK), jnp.float32)
    for slot_index in range(MAXSEL):
        _, _, scores, allowed = block_scores(
            query_blocks, key_blocks, block_rows[:, slot_index], 2 * qcount
        )
        masked = jnp.where(allowed, scores, -1e30)
        new_max = jnp.maximum(running_max, jnp.max(masked, axis=2))
        running_sum = running_sum * jnp.exp(running_max - new_max) + jnp.sum(
            jnp.where(allowed, jnp.exp(masked - new_max[:, :, None]), 0.0), axis=2
        )
        running_max = new_max
    return running_max + jnp.log(running_sum)


def tile_grads(
    query_blocks, grad_blocks, log_norm, row_delta, key_blocks, value_blocks, block_rows, key_limit
):
    qcount = query_blocks.shape[0]
    grad_query = jnp.zeros((qcount, BLK, HD), jnp.float32)
    grad_keys = jnp.zeros(key_blocks.shape, jnp.float32)
    grad_values = jnp.zeros(key_blocks.shape, jnp.float32)
    for slot_index in range(MAXSEL):
        picked, key_tiles, scores, allowed = block_scores(
            query_blocks, key_blocks, block_rows[:, slot_index], key_limit
        )
        probabilities = jnp.exp(jnp.where(allowed, scores - log_norm[:, :, None], -1e30))
        value_tiles = value_blocks[picked]
        prob_grad = jnp.einsum(
            "qid,qjd->qij", grad_blocks, value_tiles, preferred_element_type=jnp.float32
        )
        score_grad = (probabilities * (prob_grad - row_delta[:, :, None])).astype(jnp.bfloat16)
        prob_round = probabilities.astype(jnp.bfloat16)
        grad_query = grad_query + jnp.einsum(
            "qij,qjd->qid", score_grad, key_tiles, preferred_element_type=jnp.float32
        ) * HD ** (-0.5)
        grad_keys = grad_keys.at[picked].add(
            jnp.einsum("qij,qid->qjd", score_grad, query_blocks, preferred_element_type=jnp.float32)
            * HD ** (-0.5)
        )
        grad_values = grad_values.at[picked].add(
            jnp.einsum("qij,qid->qjd", prob_round, grad_blocks, preferred_element_type=jnp.float32)
        )
    return (grad_query, grad_keys, grad_values)


def shards(query_heads, key_heads, value_heads, grad_out, saved_out, block_list):
    qcount = query_heads.shape[0] // BLK
    heads_view = (
        lax.all_to_all(grad_out, "head", split_axis=1, concat_axis=0, tiled=True),
        lax.all_to_all(saved_out, "head", split_axis=1, concat_axis=0, tiled=True),
    )
    out_rows = heads_view[0]
    saved_rows = heads_view[1]
    row_delta = jnp.sum(
        out_rows.astype(jnp.float32) * saved_rows.astype(jnp.float32), axis=-1
    ).reshape(qcount, BLK)
    previous = shifted((key_heads, value_heads), "seq", 1)
    group_index = lax.axis_index("seq")
    block_rows = lax.dynamic_slice_in_dim(block_list, group_index * qcount, qcount, 0)
    query_blocks = query_heads.reshape(qcount, BLK, HD)
    grad_blocks = out_rows.reshape(qcount, BLK, HD)
    key_blocks = jnp.concatenate([previous[0], key_heads], axis=0).reshape(2 * qcount, BLK, HD)
    value_blocks = jnp.concatenate([previous[1], value_heads], axis=0).reshape(2 * qcount, BLK, HD)
    log_norm = log_totals(query_blocks, key_blocks, block_rows)
    grad_query, grad_keys, grad_values = tile_grads(
        query_blocks,
        grad_blocks,
        log_norm,
        row_delta,
        key_blocks,
        value_blocks,
        block_rows,
        2 * qcount,
    )
    returned = (
        shifted(grad_keys[:qcount].astype(jnp.bfloat16), "seq", -1).astype(jnp.float32),
        shifted(grad_values[:qcount].astype(jnp.bfloat16), "seq", -1).astype(jnp.float32),
    )
    own_keys = grad_keys[qcount:] + returned[0]
    own_values = grad_values[qcount:] + returned[1]
    result = (
        lax.all_to_all(
            grad_query.reshape(-1, HD).astype(jnp.bfloat16),
            "head",
            split_axis=0,
            concat_axis=1,
            tiled=True,
        ),
        lax.all_to_all(
            own_keys.reshape(-1, HD).astype(jnp.bfloat16),
            "head",
            split_axis=0,
            concat_axis=1,
            tiled=True,
        ),
        lax.all_to_all(
            own_values.reshape(-1, HD).astype(jnp.bfloat16),
            "head",
            split_axis=0,
            concat_axis=1,
            tiled=True,
        ),
    )
    return (result[0], result[1], result[2])


def solution(mesh):
    placed = (
        P("seq", "head"),
        P("seq", "head"),
        P("seq", "head"),
        P(("seq", "head"), None),
        P(("seq", "head"), None),
        P(),
    )
    return jax.shard_map(
        shards,
        mesh=mesh,
        in_specs=placed,
        out_specs=(P(("seq", "head"), None), P(("seq", "head"), None), P(("seq", "head"), None)),
        check_vma=False,
    )
```

profile of v0, /device:TPU:57, one launch (start us, length us, event | category | flops | bytes accessed | tf_op | source)
XLA Modules:
  0.0 262.1 jit_solution(1707244681323260644)
XLA Ops:
  0.6 3.7 %collective-permute-start.1 = (bf16[512,128]{1,0:T(8,128)(2,1)}, bf16[512,128]{1,0:T(8,128)(2,1)S(1)}, u32[]{:S(2)}, u32[]{:S(2)}) collective-permute-start(bf16[512,128]{1,0:T(8,128)(2,1)} %param.8), channel_id=1, source_target_pairs={{0,32},{32,64},{64,96},{96,128},{128,160},{160,192},{192,224},{224... | collective-permute-start | bytes 393224 | tf_op jit(solution)/shard_map/ppermute | solution.py:14
  4.3 1.6 copy_bitcast_fusion.4
  5.9 30.2 %all-to-all-start = ((bf16[16,32,128]{2,0,1:T(8,128)(2,1)}), bf16[16,32,128]{2,0,1:T(8,128)(2,1)S(1)}, u32[]{:S(2)}, u32[]{:S(2)}) async-start(bf16[16,32,128]{2,0,1:T(8,128)(2,1)} %copy_bitcast_fusion.4), calls=%async_computation | async-start | bytes 262144 | tf_op jit(solution)/shard_map/all_to_all | solution.py:85
  36.2 2.6 %collective-permute-start = (bf16[512,128]{1,0:T(8,128)(2,1)S(1)}, bf16[512,128]{1,0:T(8,128)(2,1)S(1)}, u32[]{:S(2)}, u32[]{:S(2)}) collective-permute-start(bf16[512,128]{1,0:T(8,128)(2,1)S(1)} %copy-done.28), channel_id=1, source_target_pairs={{0,32},{32,64},{64,96},{96,128},{128,160},{160,192},{192,224},{224... | collective-permute-start | bytes 393224 | tf_op jit(solution)/shard_map/ppermute | solution.py:14
  38.9 0.7 copy-done.64
  39.8 0.7 copy_bitcast_fusion.3
  40.7 2.9 %collective-permute-done = bf16[512,128]{1,0:T(8,128)(2,1)S(1)} collective-permute-done((bf16[512,128]{1,0:T(8,128)(2,1)S(1)}, bf16[512,128]{1,0:T(8,128)(2,1)S(1)}, u32[]{:S(2)}, u32[]{:S(2)}) %collective-permute-start) | collective-permute-done | bytes 131104 | tf_op jit(solution)/shard_map/ppermute | solution.py:14
  48.7 1.2 gather_fusion.8
  49.9 1.2 gather_fusion.10
  51.1 1.2 gather_fusion.11
  52.3 1.2 gather_fusion.12
  54.1 1.2 gather_fusion.13
  55.9 1.2 gather_fusion.14
  57.7 1.2 gather_fusion.15
  59.8 10.2 %all-to-all-done = bf16[16,32,128]{2,0,1:T(8,128)(2,1)S(1)} async-done(((bf16[16,32,128]{2,0,1:T(8,128)(2,1)}), bf16[16,32,128]{2,0,1:T(8,128)(2,1)S(1)}, u32[]{:S(2)}, u32[]{:S(2)}) %all-to-all-start) | async-done | bytes 131104 | tf_op jit(solution)/shard_map/all_to_all | solution.py:85
  70.0 18.1 %all-to-all-start.1 = ((bf16[16,32,128]{2,0,1:T(8,128)(2,1)}), bf16[16,32,128]{2,0,1:T(8,128)(2,1)S(1)}, u32[]{:S(2)}, u32[]{:S(2)}) async-start(bf16[16,32,128]{2,0,1:T(8,128)(2,1)} %copy_bitcast_fusion.3), calls=%async_computation.1 | async-start | bytes 262144 | tf_op jit(solution)/shard_map/all_to_all | solution.py:86
  89.2 33.1 %all-to-all-done.1 = bf16[16,32,128]{2,0,1:T(8,128)(2,1)S(1)} async-done(((bf16[16,32,128]{2,0,1:T(8,128)(2,1)}), bf16[16,32,128]{2,0,1:T(8,128)(2,1)S(1)}, u32[]{:S(2)}, u32[]{:S(2)}) %all-to-all-start.1) | async-done | bytes 131104 | tf_op jit(solution)/shard_map/all_to_all | solution.py:86
  123.0 0.9 convolution_multiply_fusion.6
  124.2 0.7 copy-done.16
  125.2 0.6 copy-done.27
  126.1 0.9 convolution_multiply_fusion.7
  127.2 0.6 copy-done.26
  128.1 0.9 convolution_multiply_fusion.5
  130.1 0.9 convolution_multiply_fusion.4
  131.2 0.6 copy-done.24
  132.1 0.9 convolution_multiply_fusion.3
  134.1 0.9 convolution_multiply_fusion.2
  136.2 0.9 convolution_multiply_fusion.1
  137.3 0.6 copy-done.21
  138.2 0.9 fusion.33
  139.1 3.6 %all-to-all-start.2 = ((bf16[32,16,128]{2,1,0:T(8,128)(2,1)}), bf16[32,16,128]{2,1,0:T(8,128)(2,1)S(1)}, u32[]{:S(2)}, u32[]{:S(2)}) async-start(bf16[32,16,128]{2,1,0:T(8,128)(2,1)} %bitcast.39), calls=%async_computation.2 | async-start | bytes 262144 | tf_op jit(solution)/shard_map/all_to_all | solution.py:118
  142.7 0.9 convolution_multiply_fusion
  143.6 0.9 copy-done.2
  144.5 1.0 scatter_fusion
  145.6 1.0 scatter_fusion.1
  146.6 1.0 scatter_fusion.2
  147.6 1.0 scatter_fusion.3
  148.7 1.0 scatter_fusion.4
  149.7 1.0 scatter_fusion.5
  150.7 1.0 scatter_fusion.6
  151.7 0.9 scatter_fusion.7
  152.6 0.7 slice.127
  153.3 1.9 collective-permute-start.2
  155.3 0.9 scatter_fusion.8
  156.2 0.9 scatter_fusion.9
  157.7 0.7 scatter_fusion.10
  159.1 0.7 scatter_fusion.11
  160.5 0.7 scatter_fusion.12
  161.3 0.7 collective-permute-done.2
  162.0 1.6 fusion.35
  163.6 11.8 %all-to-all-done.2 = bf16[32,16,128]{2,1,0:T(8,128)(2,1)S(1)} async-done(((bf16[32,16,128]{2,1,0:T(8,128)(2,1)}), bf16[32,16,128]{2,1,0:T(8,128)(2,1)S(1)}, u32[]{:S(2)}, u32[]{:S(2)}) %all-to-all-start.2) | async-done | bytes 131104 | tf_op jit(solution)/shard_map/all_to_all | solution.py:118
  175.4 11.0 %all-to-all-start.3 = ((bf16[32,16,128]{2,1,0:T(8,128)(2,1)}), bf16[32,16,128]{2,1,0:T(8,128)(2,1)S(1)}, u32[]{:S(2)}, u32[]{:S(2)}) async-start(bf16[32,16,128]{2,1,0:T(8,128)(2,1)} %bitcast.41), calls=%async_computation.3 | async-start | bytes 262144 | tf_op jit(solution)/shard_map/all_to_all | solution.py:125
  187.0 0.7 scatter_fusion.13
  188.4 0.7 scatter_fusion.14
  189.8 0.7 scatter_fusion.15
  190.6 8.9 %collective-permute-start.3 = (bf16[4,128,128]{2,1,0:T(8,128)(2,1)S(1)}, bf16[4,128,128]{2,1,0:T(8,128)(2,1)S(1)}, u32[]{:S(2)}, u32[]{:S(2)}) collective-permute-start(bf16[4,128,128]{2,1,0:T(8,128)(2,1)S(1)} %slice.126), channel_id=1, source_target_pairs={{32,0},{64,32},{96,64},{128,96},{160,128},{192,160},{224,192},{256... | collective-permute-start | bytes 393224 | tf_op jit(solution)/shard_map/ppermute | solution.py:14
  199.5 3.4 %collective-permute-done.3 = bf16[4,128,128]{2,1,0:T(8,128)(2,1)S(1)} collective-permute-done((bf16[4,128,128]{2,1,0:T(8,128)(2,1)S(1)}, bf16[4,128,128]{2,1,0:T(8,128)(2,1)S(1)}, u32[]{:S(2)}, u32[]{:S(2)}) %collective-permute-start.3) | collective-permute-done | bytes 131104 | tf_op jit(solution)/shard_map/ppermute | solution.py:14
  202.9 0.7 fusion.34
  203.6 8.8 %all-to-all-done.3 = bf16[32,16,128]{2,1,0:T(8,128)(2,1)S(1)} async-done(((bf16[32,16,128]{2,1,0:T(8,128)(2,1)}), bf16[32,16,128]{2,1,0:T(8,128)(2,1)S(1)}, u32[]{:S(2)}, u32[]{:S(2)}) %all-to-all-start.3) | async-done | bytes 131104 | tf_op jit(solution)/shard_map/all_to_all | solution.py:125
  212.4 15.3 %all-to-all-start.4 = ((bf16[32,16,128]{2,1,0:T(8,128)(2,1)}), bf16[32,16,128]{2,1,0:T(8,128)(2,1)S(1)}, u32[]{:S(2)}, u32[]{:S(2)}) async-start(bf16[32,16,128]{2,1,0:T(8,128)(2,1)} %bitcast.43), calls=%async_computation.4 | async-start | bytes 262144 | tf_op jit(solution)/shard_map/all_to_all | solution.py:132
  227.7 0.7 copy_bitcast_fusion.2
  228.3 0.7 copy_bitcast_fusion.1
  229.0 32.4 %all-to-all-done.4 = bf16[32,16,128]{2,1,0:T(8,128)(2,1)S(1)} async-done(((bf16[32,16,128]{2,1,0:T(8,128)(2,1)}), bf16[32,16,128]{2,1,0:T(8,128)(2,1)S(1)}, u32[]{:S(2)}, u32[]{:S(2)}) %all-to-all-start.4) | async-done | bytes 131104 | tf_op jit(solution)/shard_map/all_to_all | solution.py:132
  261.4 0.7 copy_bitcast_fusion
  (193 shorter events, 18.7 us)
Async XLA Ops:
  0.6 44.7 %copy-start = (bf16[512,128]{1,0:T(8,128)(2,1)S(1)}, bf16[512,128]{1,0:T(8,128)(2,1)}, u32[]{:S(2)}) copy-start(bf16[512,128]{1,0:T(8,128)(2,1)} %param.6) | copy-start | bytes 393220
  0.6 46.2 %collective-permute-start.1 = (bf16[512,128]{1,0:T(8,128)(2,1)}, bf16[512,128]{1,0:T(8,128)(2,1)S(1)}, u32[]{:S(2)}, u32[]{:S(2)}) collective-permute-start(bf16[512,128]{1,0:T(8,128)(2,1)} %param.8), channel_id=1, source_target_pairs={{0,32},{32,64},{64,96},{96,128},{128,160},{160,192},{192,224},{224... | collective-permute-start | bytes 393224 | tf_op jit(solution)/shard_map/ppermute | solution.py:14
  5.9 30.3 %copy-start.28 = (bf16[512,128]{1,0:T(8,128)(2,1)S(1)}, bf16[512,128]{1,0:T(8,128)(2,1)}, u32[]{:S(2)}) copy-start(bf16[512,128]{1,0:T(8,128)(2,1)} %param.7) | copy-start | bytes 393220
  5.9 33.8 %copy-start.20 = (bf16[16,4096]{1,0:T(8,128)(2,1)S(1)}, bf16[16,4096]{1,0:T(8,128)(2,1)}, u32[]{:S(2)}) copy-start(bf16[16,4096]{1,0:T(8,128)(2,1)} %param.10) | copy-start | bytes 393220
  5.9 64.1 %all-to-all-start = ((bf16[16,32,128]{2,0,1:T(8,128)(2,1)}), bf16[16,32,128]{2,0,1:T(8,128)(2,1)S(1)}, u32[]{:S(2)}, u32[]{:S(2)}) async-start(bf16[16,32,128]{2,0,1:T(8,128)(2,1)} %copy_bitcast_fusion.4), calls=%async_computation | async-start | bytes 262144 | tf_op jit(solution)/shard_map/all_to_all | solution.py:85
  36.2 7.4 %collective-permute-start = (bf16[512,128]{1,0:T(8,128)(2,1)S(1)}, bf16[512,128]{1,0:T(8,128)(2,1)S(1)}, u32[]{:S(2)}, u32[]{:S(2)}) collective-permute-start(bf16[512,128]{1,0:T(8,128)(2,1)S(1)} %copy-done.28), channel_id=1, source_target_pairs={{0,32},{32,64},{64,96},{96,128},{128,160},{160,192},{192,224},{224... | collective-permute-start | bytes 393224 | tf_op jit(solution)/shard_map/ppermute | solution.py:14
  39.6 0.9 copy-start.42
  39.6 0.9 copy-start.43
  39.6 0.9 copy-start.38
  39.6 0.9 copy-start.40
  39.6 0.9 copy-start.34
  39.7 0.9 copy-start.36
  39.7 0.9 copy-start.30
  39.7 0.9 copy-start.32
  39.7 87.5 %copy-start.60 = (pred[4]{0:T(512)(128)(4,1)}, pred[4]{0:T(512)(128)(4,1)S(1)}, u32[]{:S(2)}) copy-start(pred[4]{0:T(512)(128)(4,1)S(1)} %get-tuple-element.27) | copy-start | bytes 16
  39.7 87.5 %copy-start.62 = (pred[4]{0:T(512)(128)(4,1)}, pred[4]{0:T(512)(128)(4,1)S(1)}, u32[]{:S(2)}) copy-start(pred[4]{0:T(512)(128)(4,1)S(1)} %get-tuple-element.37) | copy-start | bytes 16
  39.7 89.5 %copy-start.56 = (pred[4]{0:T(512)(128)(4,1)}, pred[4]{0:T(512)(128)(4,1)S(1)}, u32[]{:S(2)}) copy-start(pred[4]{0:T(512)(128)(4,1)S(1)} %get-tuple-element.28) | copy-start | bytes 16
  39.8 89.5 %copy-start.58 = (pred[4]{0:T(512)(128)(4,1)}, pred[4]{0:T(512)(128)(4,1)S(1)}, u32[]{:S(2)}) copy-start(pred[4]{0:T(512)(128)(4,1)S(1)} %get-tuple-element.36) | copy-start | bytes 16
  39.8 91.5 %copy-start.65 = (pred[4]{0:T(512)(128)(4,1)}, pred[4]{0:T(512)(128)(4,1)S(1)}, u32[]{:S(2)}) copy-start(pred[4]{0:T(512)(128)(4,1)S(1)} %get-tuple-element.29) | copy-start | bytes 16
  39.8 91.5 %copy-start.67 = (pred[4]{0:T(512)(128)(4,1)}, pred[4]{0:T(512)(128)(4,1)S(1)}, u32[]{:S(2)}) copy-start(pred[4]{0:T(512)(128)(4,1)S(1)} %get-tuple-element.35) | copy-start | bytes 16
  39.8 93.5 %copy-start.52 = (pred[4]{0:T(512)(128)(4,1)}, pred[4]{0:T(512)(128)(4,1)S(1)}, u32[]{:S(2)}) copy-start(pred[4]{0:T(512)(128)(4,1)S(1)} %get-tuple-element.30) | copy-start | bytes 16
  39.8 93.5 %copy-start.54 = (pred[4]{0:T(512)(128)(4,1)}, pred[4]{0:T(512)(128)(4,1)S(1)}, u32[]{:S(2)}) copy-start(pred[4]{0:T(512)(128)(4,1)S(1)} %get-tuple-element.34) | copy-start | bytes 16
  39.8 95.5 %copy-start.48 = (pred[4]{0:T(512)(128)(4,1)}, pred[4]{0:T(512)(128)(4,1)S(1)}, u32[]{:S(2)}) copy-start(pred[4]{0:T(512)(128)(4,1)S(1)} %get-tuple-element.31) | copy-start | bytes 16
  39.8 95.5 %copy-start.50 = (pred[4]{0:T(512)(128)(4,1)}, pred[4]{0:T(512)(128)(4,1)S(1)}, u32[]{:S(2)}) copy-start(pred[4]{0:T(512)(128)(4,1)S(1)} %get-tuple-element.33) | copy-start | bytes 16
  39.8 97.4 %copy-start.44 = (pred[4]{0:T(512)(128)(4,1)}, pred[4]{0:T(512)(128)(4,1)S(1)}, u32[]{:S(2)}) copy-start(pred[4]{0:T(512)(128)(4,1)S(1)} %get-tuple-element.24) | copy-start | bytes 16
  39.8 97.4 %copy-start.46 = (pred[4]{0:T(512)(128)(4,1)}, pred[4]{0:T(512)(128)(4,1)S(1)}, u32[]{:S(2)}) copy-start(pred[4]{0:T(512)(128)(4,1)S(1)} %get-tuple-element.32) | copy-start | bytes 16
  44.2 2.4 copy-start.9
  46.6 0.9 copy-start.29
  46.9 12.1 %copy-start.13 = (f32[4,128,128]{1,2,0:T(8,128)}, f32[4,128,128]{1,2,0:T(8,128)S(1)}, u32[]{:S(2)}) copy-start(f32[4,128,128]{1,2,0:T(8,128)S(1)} %get-tuple-element.49) | copy-start | bytes 786436
  54.1 34.2 %copy-start.11 = (bf16[4,128,128]{2,1,0:T(8,128)(2,1)}, bf16[4,128,128]{2,1,0:T(8,128)(2,1)S(1)}, u32[]{:S(2)}) copy-start(bf16[4,128,128]{2,1,0:T(8,128)(2,1)S(1)} %gather_fusion.5) | copy-start | bytes 393220
  59.3 63.2 %copy-start.15 = (f32[4,128,128]{1,2,0:T(8,128)}, f32[4,128,128]{1,2,0:T(8,128)S(1)}, u32[]{:S(2)}) copy-start(f32[4,128,128]{1,2,0:T(8,128)S(1)} %get-tuple-element.50) | copy-start | bytes 786436
  70.0 52.3 %all-to-all-start.1 = ((bf16[16,32,128]{2,0,1:T(8,128)(2,1)}), bf16[16,32,128]{2,0,1:T(8,128)(2,1)S(1)}, u32[]{:S(2)}, u32[]{:S(2)}) async-start(bf16[16,32,128]{2,0,1:T(8,128)(2,1)} %copy_bitcast_fusion.3), calls=%async_computation.1 | async-start | bytes 262144 | tf_op jit(solution)/shard_map/all_to_all | solution.py:86
  89.2 33.3 %copy-start.17 = (f32[4,128]{1,0:T(4,128)}, f32[4,128]{1,0:T(4,128)S(1)}, u32[]{:S(2)}) copy-start(f32[4,128]{1,0:T(4,128)S(1)} %log_add_fusion) | copy-start | bytes 6148
  123.0 1.0 copy-start.14
  123.0 0.9 copy-start.18
  124.0 1.0 copy-start.16
  124.9 0.9 copy-start.27
  126.0 0.9 copy-start.10
  127.0 0.9 copy-start.26
  129.0 0.9 copy-start.25
  131.0 0.9 copy-start.24
  133.0 0.9 copy-start.23
  134.1 0.9 copy-start.12
  135.0 0.9 copy-start.22
  137.0 0.9 copy-start.21
  139.1 36.3 %all-to-all-start.2 = ((bf16[32,16,128]{2,1,0:T(8,128)(2,1)}), bf16[32,16,128]{2,1,0:T(8,128)(2,1)S(1)}, u32[]{:S(2)}, u32[]{:S(2)}) async-start(bf16[32,16,128]{2,1,0:T(8,128)(2,1)} %bitcast.39), calls=%async_computation.2 | async-start | bytes 262144 | tf_op jit(solution)/shard_map/all_to_all | solution.py:118
  143.6 0.9 copy-start.2
  144.5 1.0 copy-start.1
  145.6 1.0 copy-start.3
  146.6 1.0 copy-start.4
  147.6 1.0 copy-start.5
  148.7 1.0 copy-start.6
  149.7 1.0 copy-start.7
  150.7 1.0 copy-start.8
  153.3 8.7 %collective-permute-start.2 = (bf16[4,128,128]{2,1,0:T(8,128)(2,1)}, bf16[4,128,128]{2,1,0:T(8,128)(2,1)}, u32[]{:S(2)}, u32[]{:S(2)}) collective-permute-start(bf16[4,128,128]{2,1,0:T(8,128)(2,1)} %slice.127), channel_id=1, source_target_pairs={{32,0},{64,32},{96,64},{128,96},{160,128},{192,160},{224,192},{256... | collective-permute-start | bytes 393224 | tf_op jit(solution)/shard_map/ppermute | solution.py:14
  156.1 0.9 copy-start.19
  156.2 0.9 copy-start.61
  156.2 0.9 copy-start.63
  157.7 0.8 copy-start.59
  175.4 11.0 %copy-start.53 = (pred[4]{0:T(512)(128)(4,1)S(1)}, pred[4]{0:T(512)(128)(4,1)}, u32[]{:S(2)}) copy-start(pred[4]{0:T(512)(128)(4,1)} %copy-done.52) | copy-start | bytes 16
  175.4 11.0 %copy-start.55 = (pred[4]{0:T(512)(128)(4,1)S(1)}, pred[4]{0:T(512)(128)(4,1)}, u32[]{:S(2)}) copy-start(pred[4]{0:T(512)(128)(4,1)} %copy-done.54) | copy-start | bytes 16
  175.4 37.0 %all-to-all-start.3 = ((bf16[32,16,128]{2,1,0:T(8,128)(2,1)}), bf16[32,16,128]{2,1,0:T(8,128)(2,1)S(1)}, u32[]{:S(2)}, u32[]{:S(2)}) async-start(bf16[32,16,128]{2,1,0:T(8,128)(2,1)} %bitcast.41), calls=%async_computation.3 | async-start | bytes 262144 | tf_op jit(solution)/shard_map/all_to_all | solution.py:125
  190.6 12.3 %collective-permute-start.3 = (bf16[4,128,128]{2,1,0:T(8,128)(2,1)S(1)}, bf16[4,128,128]{2,1,0:T(8,128)(2,1)S(1)}, u32[]{:S(2)}, u32[]{:S(2)}) collective-permute-start(bf16[4,128,128]{2,1,0:T(8,128)(2,1)S(1)} %slice.126), channel_id=1, source_target_pairs={{32,0},{64,32},{96,64},{128,96},{160,128},{192,160},{224,192},{256... | collective-permute-start | bytes 393224 | tf_op jit(solution)/shard_map/ppermute | solution.py:14
  212.4 49.0 %all-to-all-start.4 = ((bf16[32,16,128]{2,1,0:T(8,128)(2,1)}), bf16[32,16,128]{2,1,0:T(8,128)(2,1)S(1)}, u32[]{:S(2)}, u32[]{:S(2)}) async-start(bf16[32,16,128]{2,1,0:T(8,128)(2,1)} %bitcast.43), calls=%async_computation.4 | async-start | bytes 262144 | tf_op jit(solution)/shard_map/all_to_all | solution.py:132
  (14 other events, 9.7 us)
where the time goes:
time: 263 us; the launch traced here: 262 us
  waiting for transfers between devices  103 us (39%)
  starting transfers between devices  95.4 us (36%)
  local copies, waits for them, and re-layouts  28.5 us (11%)
  other arithmetic  17.3 us (7%)
  matrix products  15.5 us (6%)
    all_to_all x1, waiting for transfers between devices, shards(): lax.all_to_all(saved_out, 'head', split_axis=1, concat_axis=0, tiled=True)  33.1 us
    all_to_all x1, waiting for transfers between devices, shards(): lax.all_to_all(own_values.reshape(-1, HD).astype(jnp.bfloat16), 'head', s...  32.4 us
    all_to_all x1, starting transfers between devices, shards(): lax.all_to_all(grad_out, 'head', split_axis=1, concat_axis=0, tiled=True)  30.2 us
    all_to_all x1, starting transfers between devices, shards(): lax.all_to_all(saved_out, 'head', split_axis=1, concat_axis=0, tiled=True)  18.1 us
    ppermute x4, starting transfers between devices, shifted(): return lax.ppermute(value, axis, pairs)  17.1 us
    all_to_all x1, starting transfers between devices, shards(): lax.all_to_all(own_values.reshape(-1, HD).astype(jnp.bfloat16), 'head', s...  15.3 us
    all_to_all x1, waiting for transfers between devices, shards(): lax.all_to_all(grad_query.reshape(-1, HD).astype(jnp.bfloat16), 'head', s...  11.8 us
    all_to_all x1, starting transfers between devices, shards(): lax.all_to_all(own_keys.reshape(-1, HD).astype(jnp.bfloat16), 'head', spl...  11 us
  transfers between devices with their start and end apart: 9, of which 8 were waited for; matrix products, arithmetic and copies ran while one was open for 15% of the time, Pallas kernels for 0%

commit v1 on v0

v1 whole, which is shorter than its diff:
```python
import functools

import jax
import jax.numpy as jnp
from jax import lax
from jax.experimental import pallas as pl
from jax.experimental.pallas import tpu as pltpu
from jax.sharding import PartitionSpec as P

HD = 128
BLK = 128
MAXSEL = 8
SCALE = HD ** (-0.5)
MASKED = -1e30
LIMIT = 24 * 1024 * 1024
VM = pl.BlockSpec(memory_space=pltpu.VMEM)
SM = pl.BlockSpec(memory_space=pltpu.SMEM)
F32 = jnp.float32
BF16 = jnp.bfloat16


def shifted(value, axis, by):
    size = lax.axis_size(axis)
    pairs = [(i, i + by) for i in range(size) if 0 <= i + by < size]
    return lax.ppermute(value, axis, pairs)


def nt(a, b):
    return lax.dot_general(a, b, (((1,), (1,)), ((), ())), preferred_element_type=F32)


def nn(a, b):
    return lax.dot_general(a, b, (((1,), (0,)), ((), ())), preferred_element_type=F32)


def tn(a, b):
    return lax.dot_general(a, b, (((0,), (0,)), ((), ())), preferred_element_type=F32)


def call(body, ins, outs, name, flops, nbytes, scratch=()):
    return pl.pallas_call(
        body,
        in_specs=ins,
        out_specs=tuple(VM for _ in outs),
        out_shape=tuple(jax.ShapeDtypeStruct(s, d) for s, d in outs),
        scratch_shapes=list(scratch),
        compiler_params=pltpu.CompilerParams(vmem_limit_bytes=LIMIT),
        cost_estimate=pl.CostEstimate(flops=flops, bytes_accessed=nbytes, transcendentals=0),
        name=name,
    )


def pack_kernel(slot_ref, grad_ref, saved_ref, out_ref, square):
    heads, rows = out_ref.shape[0], grad_ref.shape[0]
    lane = lax.broadcasted_iota(jnp.int32, (rows, BLK), 1)
    delta = jnp.zeros((rows, BLK), F32)
    for h in range(heads):
        g = grad_ref[:, h * HD : (h + 1) * HD]
        out_ref[h, 0:rows, :] = g
        prod = g.astype(F32) * saved_ref[:, h * HD : (h + 1) * HD].astype(F32)
        delta = jnp.where(lane == h, jnp.sum(prod, axis=1, keepdims=True), delta)
    square[...] = jnp.zeros_like(square)
    start = pl.multiple_of(slot_ref[0] * rows, rows)
    square[pl.ds(start, rows), :] = delta
    turned = square[...].T
    high = turned.astype(BF16).astype(F32)
    rest = turned - high
    mid = rest.astype(BF16).astype(F32)
    low = rest - mid
    row = lax.broadcasted_iota(jnp.int32, (8, BLK), 0)
    for h in range(heads):
        parts = jnp.where(row == 0, high[h : h + 1, :], 0.0)
        parts = jnp.where(row == 1, mid[h : h + 1, :], parts)
        parts = jnp.where(row == 2, low[h : h + 1, :], parts)
        out_ref[h, rows : rows + 8, :] = parts.astype(BF16)


def prob_kernel(list_ref, q_ref, k_ref, prev_ref, p_ref):
    span = q_ref.shape[0]
    qcount = span // BLK
    listed = []
    for b in range(qcount):
        bits = jnp.int32(0)
        for slot in range(MAXSEL):
            entry = list_ref[b, slot]
            bits = bits | jnp.where(entry >= 0, jnp.int32(1) << jnp.maximum(entry, 0), 0)
        listed.append(bits)
    lane = lax.broadcasted_iota(jnp.int32, (1, 2 * BLK), 1)
    key_row = lax.broadcasted_iota(jnp.int32, (BLK, 2 * BLK), 0)
    query_col = lax.broadcasted_iota(jnp.int32, (BLK, 2 * BLK), 1)
    for pair in range(qcount // 2):
        first = 2 * pair
        cols = slice(first * BLK, (first + 2) * BLK)
        queries = q_ref[cols, :]
        bits = jnp.where(lane < BLK, listed[first], listed[first + 1])
        keys_of = [(j, prev_ref[j * BLK : (j + 1) * BLK, :]) for j in range(qcount)]
        keys_of += [
            (qcount + j, k_ref[j * BLK : (j + 1) * BLK, :]) for j in range(first + 2)
        ]
        top = jnp.full((BLK, 2 * BLK), MASKED, F32)
        for j, keys in keys_of:
            scores = nt(keys, queries) * SCALE
            allowed = jnp.broadcast_to(((bits >> j) & 1) == 1, scores.shape)
            if j >= qcount + first:
                own = (j - qcount - first) * BLK
                inside = (query_col >= own) & (query_col < own + BLK)
                allowed = allowed & (jnp.logical_not(inside) | (key_row <= query_col - own))
            scores = jnp.where(allowed, scores, MASKED)
            p_ref[j * BLK : (j + 1) * BLK, cols] = scores
            top = jnp.maximum(top, scores)
        top = jnp.max(top, axis=0, keepdims=True)
        total = jnp.zeros((BLK, 2 * BLK), F32)
        for j, _ in keys_of:
            e = jnp.exp(p_ref[j * BLK : (j + 1) * BLK, cols] - top)
            p_ref[j * BLK : (j + 1) * BLK, cols] = e
            total = total + e
        inverse = 1.0 / jnp.sum(total, axis=0, keepdims=True)
        for j, _ in keys_of:
            p_ref[j * BLK : (j + 1) * BLK, cols] = p_ref[j * BLK : (j + 1) * BLK, cols] * inverse
        for j in range(first + 2, qcount):
            rows = slice((qcount + j) * BLK, (qcount + j + 1) * BLK)
            p_ref[rows, cols] = jnp.zeros((BLK, 2 * BLK), F32)


def received(recv_ref):
    peers, slab = recv_ref.shape[0], recv_ref.shape[1]
    rows = slab - 8
    grads = recv_ref[:, 0:rows, :].reshape(peers * rows, HD)
    parts = recv_ref[:, rows:slab, :].astype(F32)
    each = BLK // rows
    deltas = [
        jnp.sum(jnp.sum(parts[b * each : (b + 1) * each], axis=0), axis=0, keepdims=True)
        for b in range(peers // each)
    ]
    return grads, deltas


def prev_kernel(p_ref, recv_ref, q_ref, prev_ref, back_ref, dq_ref):
    span = q_ref.shape[0]
    grads, deltas = received(recv_ref)
    delta = jnp.concatenate(deltas, axis=1)
    keys, values = prev_ref[0:span, :], prev_ref[span : 2 * span, :]
    p = p_ref[0:span, :]
    score_grad = (p * (nt(values, grads) - delta)).astype(BF16)
    back_ref[0:span, :] = (nn(score_grad, q_ref[...]) * SCALE).astype(BF16)
    back_ref[span : 2 * span, :] = nn(p.astype(BF16), grads).astype(BF16)
    dq_ref[...] = tn(score_grad, keys)


def own_kernel(p_ref, recv_ref, q_ref, k_ref, v_ref, part_ref, dq_ref, dkv_ref):
    span = q_ref.shape[0]
    grads, deltas = received(recv_ref)
    delta = jnp.concatenate(deltas, axis=1)
    p = p_ref[span : 2 * span, :]
    score_grad = (p * (nt(v_ref[...], grads) - delta)).astype(BF16)
    dkv_ref[0:span, :] = nn(score_grad, q_ref[...]) * SCALE
    dkv_ref[span : 2 * span, :] = nn(p.astype(BF16), grads)
    dq_ref[...] = ((part_ref[...] + tn(score_grad, k_ref[...])) * SCALE).astype(BF16)


def join_kernel(dq_ref, dkv_ref, back_ref, out_ref):
    peers, rows = out_ref.shape[0], out_ref.shape[1] // 3
    span = dq_ref.shape[0]
    out_ref[:, 0:rows, :] = dq_ref[...].reshape(peers, rows, HD)
    both = (dkv_ref[...] + back_ref[...].astype(F32)).astype(BF16)
    out_ref[:, rows : 2 * rows, :] = both[0:span].reshape(peers, rows, HD)
    out_ref[:, 2 * rows : 3 * rows, :] = both[span:].reshape(peers, rows, HD)


def split_kernel(in_ref, dq_ref, dk_ref, dv_ref):
    peers, rows = in_ref.shape[0], in_ref.shape[1] // 3
    for h in range(peers):
        for i, ref in enumerate((dq_ref, dk_ref, dv_ref)):
            ref[:, h * HD : (h + 1) * HD] = in_ref[h, i * rows : (i + 1) * rows, :]


def shards(query_heads, key_heads, value_heads, grad_out, saved_out, block_list):
    span = query_heads.shape[0]
    qcount = span // BLK
    heads = lax.axis_size("head")
    rows = grad_out.shape[0]
    slot = lax.rem(lax.axis_index("head"), BLK // rows).astype(jnp.int32)[None]
    (packed,) = call(
        pack_kernel,
        [SM, VM, VM],
        [((heads, rows + 8, HD), BF16)],
        "pack",
        4 * rows * heads * HD,
        6 * rows * heads * HD,
        [pltpu.VMEM((BLK, BLK), F32)],
    )(slot, grad_out, saved_out)
    arrived = lax.all_to_all(packed, "head", split_axis=0, concat_axis=0, tiled=True)
    previous = shifted(jnp.concatenate([key_heads, value_heads], axis=0), "seq", 1)
    group_index = lax.axis_index("seq")
    block_rows = lax.dynamic_slice_in_dim(block_list, group_index * qcount, qcount, 0)
    (probs,) = call(
        prob_kernel,
        [SM, VM, VM, VM],
        [((2 * span, span), F32)],
        "probs",
        4 * span * span * HD,
        12 * span * span,
    )(block_rows, query_heads, key_heads, previous)
    back, dq_part = call(
        prev_kernel,
        [VM] * 4,
        [((2 * span, HD), BF16), ((span, HD), F32)],
        "prev_grads",
        8 * span * span * HD,
        8 * span * span,
    )(probs, arrived, query_heads, previous)
    returned = shifted(back, "seq", -1)
    grad_query, own = call(
        own_kernel,
        [VM] * 6,
        [((span, HD), BF16), ((2 * span, HD), F32)],
        "own_grads",
        8 * span * span * HD,
        8 * span * span,
    )(probs, arrived, query_heads, key_heads, value_heads, dq_part)
    (joined,) = call(
        join_kernel,
        [VM] * 3,
        [((heads, 3 * rows, HD), BF16)],
        "join",
        4 * span * HD,
        16 * span * HD,
    )(grad_query, own, returned)
    landed = lax.all_to_all(joined, "head", split_axis=0, concat_axis=0, tiled=True)
    return call(
        split_kernel,
        [VM],
        [((rows, heads * HD), BF16)] * 3,
        "split",
        0,
        12 * rows * heads * HD,
    )(landed)


def solution(mesh):
    placed = (
        P("seq", "head"),
        P("seq", "head"),
        P("seq", "head"),
        P(("seq", "head"), None),
        P(("seq", "head"), None),
        P(),
    )
    return jax.shard_map(
        shards,
        mesh=mesh,
        in_specs=placed,
        out_specs=(P(("seq", "head"), None), P(("seq", "head"), None), P(("seq", "head"), None)),
        check_vma=False,
    )
```

time: 263 us -> 150 us (0.57)
  the two profiles are of different devices: /device:TPU:57 before, /device:TPU:105 now
where the time goes in v1:
time: 150 us; the launch traced here: 149 us
  blocking collectives  62.9 us (42%)
  waiting for transfers between devices  42.6 us (28%)
  starting transfers between devices  33.5 us (22%)
  Pallas kernels  4.9 us (3%)
  local copies, waits for them, and re-layouts  3.83 us (3%)
    all_to_all x1, blocking collectives, shards(): lax.all_to_all(joined, 'head', split_axis=0, concat_axis=0, tiled=True)  62.9 us
    all_to_all x1, starting transfers between devices, shards(): lax.all_to_all(packed, 'head', split_axis=0, concat_axis=0, tiled=True)  28.9 us
    ppermute x2, waiting for transfers between devices, shifted(): return lax.ppermute(value, axis, pairs)  27.8 us
    all_to_all x1, waiting for transfers between devices, shards(): lax.all_to_all(packed, 'head', split_axis=0, concat_axis=0, tiled=True)  14.8 us
    ppermute x2, starting transfers between devices, shifted(): return lax.ppermute(value, axis, pairs)  4.57 us
    unnamed x17, local copies, waits for them, and re-layouts  3.75 us
  transfers between devices with their start and end apart: 3, of which 3 were waited for; matrix products, arithmetic and copies ran while one was open for 1% of the time, Pallas kernels for 2%

profile of v1, /device:TPU:105, one launch (start us, length us, event | category | flops | bytes accessed | tf_op | source)
XLA Modules:
  0.0 149.4 jit_solution(683892766269186439)
XLA Ops:
  0.6 0.0 copy-start
  0.6 0.0 copy-start.4
  0.7 0.0 copy-start.6
  0.7 0.9 copy-done.6
  1.6 0.0 copy-start.7
  1.6 0.9 copy-done.7
  2.5 0.9 pack.1
  3.4 28.9 %all-to-all-start = ((bf16[32,24,128]{2,1,0:T(8,128)(2,1)}), bf16[32,24,128]{2,1,0:T(8,128)(2,1)S(1)}, u32[]{:S(2)}, u32[]{:S(2)}) async-start(bf16[32,24,128]{2,1,0:T(8,128)(2,1)} %pack.1), calls=%async_computation | async-start | bytes 393216 | tf_op jit(solution)/shard_map/all_to_all | solution.py:192
  32.4 1.0 pad_maximum_fusion
  33.4 2.6 %collective-permute-start = (bf16[1024,128]{1,0:T(8,128)(2,1)S(1)}, bf16[1024,128]{1,0:T(8,128)(2,1)S(1)}, u32[]{:S(2)}, u32[]{:S(2)}) collective-permute-start(bf16[1024,128]{1,0:T(8,128)(2,1)S(1)} %pad_maximum_fusion), channel_id=1, source_target_pairs={{0,32},{32,64},{64,96},{96,128},{128,160},{160,192},{192,224},{224... | collective-permute-start | bytes 786440 | tf_op jit(solution)/shard_map/ppermute | solution.py:25
  36.0 0.0 copy-done
  36.1 0.1 constant_dynamic-slice_fusion
  36.1 0.1 copy.10.list_ref
  36.2 19.4 %collective-permute-done.prev_ref = bf16[1024,128]{1,0:T(8,128)(2,1)S(1)} collective-permute-done((bf16[1024,128]{1,0:T(8,128)(2,1)S(1)}, bf16[1024,128]{1,0:T(8,128)(2,1)S(1)}, u32[]{:S(2)}, u32[]{:S(2)}) %collective-permute-start) | collective-permute-done | bytes 262176 | tf_op jit(solution)/shard_map/ppermute | solution.py:25
  55.6 0.0 copy-start.1
  55.6 0.9 copy-done.1
  56.5 0.0 copy-start.3
  56.5 0.9 copy-done.3
  57.4 0.0 copy-start.2
  57.4 0.0 copy-start.5
  57.4 1.5 %probs.1.p_ref = f32[1024,512]{1,0:T(8,128)S(1)} custom-call(s32[4,8]{1,0:T(4,128)S(1)} %copy.10.list_ref, bf16[512,128]{1,0:T(8,128)(2,1)S(1)} %copy-done.3, bf16[512,128]{1,0:T(8,128)(2,1)S(1)} %copy-done.1, bf16[1024,128]{1,0:T(8,128)(2,1)S(1)} %collective-permute-done.prev_ref), custom_call_target="tpu_custom_call" | custom-call | flops 134217728 | bytes 3145728 | tf_op jit(solution)/shard_map/probs/pallas_call | solution.py:196
  58.9 14.8 %all-to-all-done.recv_ref = bf16[32,24,128]{2,1,0:T(8,128)(2,1)S(1)} async-done(((bf16[32,24,128]{2,1,0:T(8,128)(2,1)}), bf16[32,24,128]{2,1,0:T(8,128)(2,1)S(1)}, u32[]{:S(2)}, u32[]{:S(2)}) %all-to-all-start) | async-done | bytes 196640 | tf_op jit(solution)/shard_map/all_to_all | solution.py:192
  73.7 0.0 copy-done.4
  73.7 0.8 prev_grads.1
  74.5 1.9 %collective-permute-start.1 = (bf16[1024,128]{1,0:T(8,128)(2,1)S(1)}, bf16[1024,128]{1,0:T(8,128)(2,1)S(1)}, u32[]{:S(2)}, u32[]{:S(2)}) collective-permute-start(bf16[1024,128]{1,0:T(8,128)(2,1)S(1)} %get-tuple-element.10), channel_id=1, source_target_pairs={{32,0},{64,32},{96,64},{128,96},{160,128},{192,160},{224,192},{256... | collective-permute-start | bytes 786440 | tf_op jit(solution)/shard_map/ppermute | solution.py:25
  76.5 0.0 copy-done.2
  76.5 0.0 copy-done.5
  76.5 0.7 own_grads.1
  77.2 8.4 %collective-permute-done.1.back_ref = bf16[1024,128]{1,0:T(8,128)(2,1)S(1)} collective-permute-done((bf16[1024,128]{1,0:T(8,128)(2,1)S(1)}, bf16[1024,128]{1,0:T(8,128)(2,1)S(1)}, u32[]{:S(2)}, u32[]{:S(2)}) %collective-permute-start.1) | collective-permute-done | bytes 262176 | tf_op jit(solution)/shard_map/ppermute | solution.py:25
  85.6 0.1 join.1
  85.7 62.9 %all_to_all.10.in_ref = bf16[32,48,128]{2,1,0:T(8,128)(2,1)S(1)} all-to-all(bf16[32,48,128]{2,1,0:T(8,128)(2,1)S(1)} %join.1), channel_id=1, replica_groups=mesh['seq'=32,'head'=32] {'head'}, dimensions={0} | all-to-all | bytes 786432 | tf_op jit(solution)/shard_map/all_to_all | solution.py:229
  148.6 0.8 split.1
Async XLA Ops:
  0.6 35.4 %copy-start = (s32[128,8]{0,1:T(8,128)S(1)}, s32[128,8]{0,1:T(8,128)}, u32[]{:S(2)}) copy-start(s32[128,8]{0,1:T(8,128)} %param.11) | copy-start | bytes 12292
  0.6 73.1 %copy-start.4 = (bf16[512,128]{1,0:T(8,128)(2,1)S(1)}, bf16[512,128]{1,0:T(8,128)(2,1)}, u32[]{:S(2)}) copy-start(bf16[512,128]{1,0:T(8,128)(2,1)} %q_ref.5) | copy-start | bytes 393220
  0.7 0.9 copy-start.6
  1.6 0.9 copy-start.7
  3.4 70.3 %all-to-all-start = ((bf16[32,24,128]{2,1,0:T(8,128)(2,1)}), bf16[32,24,128]{2,1,0:T(8,128)(2,1)S(1)}, u32[]{:S(2)}, u32[]{:S(2)}) async-start(bf16[32,24,128]{2,1,0:T(8,128)(2,1)} %pack.1), calls=%async_computation | async-start | bytes 393216 | tf_op jit(solution)/shard_map/all_to_all | solution.py:192
  33.4 22.2 %collective-permute-start = (bf16[1024,128]{1,0:T(8,128)(2,1)S(1)}, bf16[1024,128]{1,0:T(8,128)(2,1)S(1)}, u32[]{:S(2)}, u32[]{:S(2)}) collective-permute-start(bf16[1024,128]{1,0:T(8,128)(2,1)S(1)} %pad_maximum_fusion), channel_id=1, source_target_pairs={{0,32},{32,64},{64,96},{96,128},{128,160},{160,192},{192,224},{224... | collective-permute-start | bytes 786440 | tf_op jit(solution)/shard_map/ppermute | solution.py:25
  55.6 0.9 copy-start.1
  56.5 0.9 copy-start.3
  57.4 19.1 %copy-start.2 = (bf16[512,128]{1,0:T(8,128)(2,1)S(1)}, bf16[512,128]{1,0:T(8,128)(2,1)}, u32[]{:S(2)}) copy-start(bf16[512,128]{1,0:T(8,128)(2,1)} %k_ref.3) | copy-start | bytes 393220
  57.4 19.1 %copy-start.5 = (bf16[512,128]{1,0:T(8,128)(2,1)S(1)}, bf16[512,128]{1,0:T(8,128)(2,1)}, u32[]{:S(2)}) copy-start(bf16[512,128]{1,0:T(8,128)(2,1)} %v_ref.1) | copy-start | bytes 393220
  74.5 11.1 %collective-permute-start.1 = (bf16[1024,128]{1,0:T(8,128)(2,1)S(1)}, bf16[1024,128]{1,0:T(8,128)(2,1)S(1)}, u32[]{:S(2)}, u32[]{:S(2)}) collective-permute-start(bf16[1024,128]{1,0:T(8,128)(2,1)S(1)} %get-tuple-element.10), channel_id=1, source_target_pairs={{32,0},{64,32},{96,64},{128,96},{160,128},{192,160},{224,192},{256... | collective-permute-start | bytes 786440 | tf_op jit(solution)/shard_map/ppermute | solution.py:25

commit v2 on v1

--- a/solution.py
+++ b/solution.py
@@ -56,7 +56,8 @@
     delta = jnp.zeros((rows, BLK), F32)
     for h in range(heads):
         g = grad_ref[:, h * HD : (h + 1) * HD]
-        out_ref[h, 0:rows, :] = g
+        for k in range(rows // 2):
+            out_ref[h, k] = g[2 * k : 2 * k + 2, :]
         prod = g.astype(F32) * saved_ref[:, h * HD : (h + 1) * HD].astype(F32)
         delta = jnp.where(lane == h, jnp.sum(prod, axis=1, keepdims=True), delta)
     square[...] = jnp.zeros_like(square)
@@ -65,14 +66,10 @@
     turned = square[...].T
     high = turned.astype(BF16).astype(F32)
     rest = turned - high
-    mid = rest.astype(BF16).astype(F32)
-    low = rest - mid
-    row = lax.broadcasted_iota(jnp.int32, (8, BLK), 0)
+    row = lax.broadcasted_iota(jnp.int32, (2, BLK), 0)
     for h in range(heads):
-        parts = jnp.where(row == 0, high[h : h + 1, :], 0.0)
-        parts = jnp.where(row == 1, mid[h : h + 1, :], parts)
-        parts = jnp.where(row == 2, low[h : h + 1, :], parts)
-        out_ref[h, rows : rows + 8, :] = parts.astype(BF16)
+        parts = jnp.where(row == 0, high[h : h + 1, :], rest[h : h + 1, :])
+        out_ref[h, rows // 2] = parts.astype(BF16)
 
 
 def prob_kernel(list_ref, q_ref, k_ref, prev_ref, p_ref):
@@ -123,13 +120,13 @@
 
 
 def received(recv_ref):
-    peers, slab = recv_ref.shape[0], recv_ref.shape[1]
-    rows = slab - 8
-    grads = recv_ref[:, 0:rows, :].reshape(peers * rows, HD)
-    parts = recv_ref[:, rows:slab, :].astype(F32)
+    peers, pairs = recv_ref.shape[0], recv_ref.shape[1] - 1
+    rows = 2 * pairs
+    grads = recv_ref[:, 0:pairs].reshape(peers * rows, HD)
+    parts = jnp.sum(recv_ref[:, pairs].astype(F32), axis=1)
     each = BLK // rows
     deltas = [
-        jnp.sum(jnp.sum(parts[b * each : (b + 1) * each], axis=0), axis=0, keepdims=True)
+        jnp.sum(parts[b * each : (b + 1) * each], axis=0, keepdims=True)
         for b in range(peers // each)
     ]
     return grads, deltas
@@ -183,7 +180,7 @@
     (packed,) = call(
         pack_kernel,
         [SM, VM, VM],
-        [((heads, rows + 8, HD), BF16)],
+        [((heads, rows // 2 + 1, 2, HD), BF16)],
         "pack",
         4 * rows * heads * HD,
         6 * rows * heads * HD,

time: 150 us -> 147 us (0.980)
  the two profiles are of different devices: /device:TPU:105 before, /device:TPU:57 now
where the time goes in v2:
time: 147 us; the launch traced here: 145 us
  blocking collectives  65.8 us (45%)
  starting transfers between devices  35.3 us (24%)
  waiting for transfers between devices  33.7 us (23%)
  Pallas kernels  4.94 us (3%)
  local copies, waits for them, and re-layouts  3.83 us (3%)
    all_to_all x1, blocking collectives, shards(): lax.all_to_all(joined, 'head', split_axis=0, concat_axis=0, tiled=True)  65.8 us
    all_to_all x1, starting transfers between devices, shards(): lax.all_to_all(packed, 'head', split_axis=0, concat_axis=0, tiled=True)  30.7 us
    ppermute x2, waiting for transfers between devices, shifted(): return lax.ppermute(value, axis, pairs)  21.7 us
    all_to_all x1, waiting for transfers between devices, shards(): lax.all_to_all(packed, 'head', split_axis=0, concat_axis=0, tiled=True)  12 us
    ppermute x2, starting transfers between devices, shifted(): return lax.ppermute(value, axis, pairs)  4.57 us
    unnamed x17, local copies, waits for them, and re-layouts  3.75 us
  transfers between devices with their start and end apart: 3, of which 3 were waited for; matrix products, arithmetic and copies ran while one was open for 1% of the time, Pallas kernels for 2%

profile of v2, /device:TPU:57, one launch (start us, length us, event | category | flops | bytes accessed | tf_op | source)
XLA Modules:
  0.0 145.3 jit_solution(7855036926315407467)
XLA Ops:
  0.6 0.0 copy-start
  0.6 0.0 copy-start.2
  0.7 0.0 copy-start.6
  0.7 0.9 copy-done.6
  1.6 0.0 copy-start.7
  1.6 0.9 copy-done.7
  2.5 0.9 pack.1
  3.4 30.7 %all-to-all-start = ((bf16[32,9,2,128]{3,2,1,0:T(2,128)(2,1)}), bf16[32,9,2,128]{3,2,1,0:T(2,128)(2,1)S(1)}, u32[]{:S(2)}, u32[]{:S(2)}) async-start(bf16[32,9,2,128]{3,2,1,0:T(2,128)(2,1)} %pack.1), calls=%async_computation | async-start | bytes 294912 | tf_op jit(solution)/shard_map/all_to_all | solution.py:189
  34.2 1.0 pad_maximum_fusion
  35.2 2.6 %collective-permute-start = (bf16[1024,128]{1,0:T(8,128)(2,1)S(1)}, bf16[1024,128]{1,0:T(8,128)(2,1)S(1)}, u32[]{:S(2)}, u32[]{:S(2)}) collective-permute-start(bf16[1024,128]{1,0:T(8,128)(2,1)S(1)} %pad_maximum_fusion), channel_id=1, source_target_pairs={{0,32},{32,64},{64,96},{96,128},{128,160},{160,192},{192,224},{224... | collective-permute-start | bytes 786440 | tf_op jit(solution)/shard_map/ppermute | solution.py:25
  37.8 0.0 copy-done
  37.8 0.1 constant_dynamic-slice_fusion
  37.9 0.1 copy.10.list_ref
  38.0 16.0 %collective-permute-done.prev_ref = bf16[1024,128]{1,0:T(8,128)(2,1)S(1)} collective-permute-done((bf16[1024,128]{1,0:T(8,128)(2,1)S(1)}, bf16[1024,128]{1,0:T(8,128)(2,1)S(1)}, u32[]{:S(2)}, u32[]{:S(2)}) %collective-permute-start) | collective-permute-done | bytes 262176 | tf_op jit(solution)/shard_map/ppermute | solution.py:25
  54.0 0.0 copy-start.1
  54.0 0.9 copy-done.1
  54.9 0.0 copy-start.3
  54.9 0.9 copy-done.3
  55.8 0.0 copy-start.4
  55.8 0.0 copy-start.5
  55.8 1.5 %probs.1.p_ref = f32[1024,512]{1,0:T(8,128)S(1)} custom-call(s32[4,8]{1,0:T(4,128)S(1)} %copy.10.list_ref, bf16[512,128]{1,0:T(8,128)(2,1)S(1)} %copy-done.1, bf16[512,128]{1,0:T(8,128)(2,1)S(1)} %copy-done.3, bf16[1024,128]{1,0:T(8,128)(2,1)S(1)} %collective-permute-done.prev_ref), custom_call_target="tpu_custom_call" | custom-call | flops 134217728 | bytes 3145728 | tf_op jit(solution)/shard_map/probs/pallas_call | solution.py:193
  57.4 12.0 %all-to-all-done.recv_ref = bf16[32,9,2,128]{3,2,1,0:T(2,128)(2,1)S(1)} async-done(((bf16[32,9,2,128]{3,2,1,0:T(2,128)(2,1)}), bf16[32,9,2,128]{3,2,1,0:T(2,128)(2,1)S(1)}, u32[]{:S(2)}, u32[]{:S(2)}) %all-to-all-start) | async-done | bytes 147488 | tf_op jit(solution)/shard_map/all_to_all | solution.py:189
  69.4 0.0 copy-done.2
  69.4 0.8 prev_grads.1
  70.2 1.9 %collective-permute-start.1 = (bf16[1024,128]{1,0:T(8,128)(2,1)S(1)}, bf16[1024,128]{1,0:T(8,128)(2,1)S(1)}, u32[]{:S(2)}, u32[]{:S(2)}) collective-permute-start(bf16[1024,128]{1,0:T(8,128)(2,1)S(1)} %get-tuple-element.10), channel_id=1, source_target_pairs={{32,0},{64,32},{96,64},{128,96},{160,128},{192,160},{224,192},{256... | collective-permute-start | bytes 786440 | tf_op jit(solution)/shard_map/ppermute | solution.py:25
  72.1 0.0 copy-done.4
  72.1 0.0 copy-done.5
  72.1 0.8 own_grads.1
  72.9 5.7 %collective-permute-done.1.back_ref = bf16[1024,128]{1,0:T(8,128)(2,1)S(1)} collective-permute-done((bf16[1024,128]{1,0:T(8,128)(2,1)S(1)}, bf16[1024,128]{1,0:T(8,128)(2,1)S(1)}, u32[]{:S(2)}, u32[]{:S(2)}) %collective-permute-start.1) | collective-permute-done | bytes 262176 | tf_op jit(solution)/shard_map/ppermute | solution.py:25
  78.7 0.1 join.1
  78.7 65.8 %all_to_all.10.in_ref = bf16[32,48,128]{2,1,0:T(8,128)(2,1)S(1)} all-to-all(bf16[32,48,128]{2,1,0:T(8,128)(2,1)S(1)} %join.1), channel_id=1, replica_groups=mesh['seq'=32,'head'=32] {'head'}, dimensions={0} | all-to-all | bytes 786432 | tf_op jit(solution)/shard_map/all_to_all | solution.py:226
  144.5 0.8 split.1
Async XLA Ops:
  0.6 37.2 %copy-start = (s32[128,8]{0,1:T(8,128)S(1)}, s32[128,8]{0,1:T(8,128)}, u32[]{:S(2)}) copy-start(s32[128,8]{0,1:T(8,128)} %param.11) | copy-start | bytes 12292
  0.6 68.7 %copy-start.2 = (bf16[512,128]{1,0:T(8,128)(2,1)S(1)}, bf16[512,128]{1,0:T(8,128)(2,1)}, u32[]{:S(2)}) copy-start(bf16[512,128]{1,0:T(8,128)(2,1)} %q_ref.5) | copy-start | bytes 393220
  0.7 0.9 copy-start.6
  1.6 0.9 copy-start.7
  3.4 65.9 %all-to-all-start = ((bf16[32,9,2,128]{3,2,1,0:T(2,128)(2,1)}), bf16[32,9,2,128]{3,2,1,0:T(2,128)(2,1)S(1)}, u32[]{:S(2)}, u32[]{:S(2)}) async-start(bf16[32,9,2,128]{3,2,1,0:T(2,128)(2,1)} %pack.1), calls=%async_computation | async-start | bytes 294912 | tf_op jit(solution)/shard_map/all_to_all | solution.py:189
  35.2 18.8 %collective-permute-start = (bf16[1024,128]{1,0:T(8,128)(2,1)S(1)}, bf16[1024,128]{1,0:T(8,128)(2,1)S(1)}, u32[]{:S(2)}, u32[]{:S(2)}) collective-permute-start(bf16[1024,128]{1,0:T(8,128)(2,1)S(1)} %pad_maximum_fusion), channel_id=1, source_target_pairs={{0,32},{32,64},{64,96},{96,128},{128,160},{160,192},{192,224},{224... | collective-permute-start | bytes 786440 | tf_op jit(solution)/shard_map/ppermute | solution.py:25
  54.0 0.9 copy-start.1
  54.9 0.9 copy-start.3
  55.8 16.3 %copy-start.4 = (bf16[512,128]{1,0:T(8,128)(2,1)S(1)}, bf16[512,128]{1,0:T(8,128)(2,1)}, u32[]{:S(2)}) copy-start(bf16[512,128]{1,0:T(8,128)(2,1)} %k_ref.3) | copy-start | bytes 393220
  55.8 16.3 %copy-start.5 = (bf16[512,128]{1,0:T(8,128)(2,1)S(1)}, bf16[512,128]{1,0:T(8,128)(2,1)}, u32[]{:S(2)}) copy-start(bf16[512,128]{1,0:T(8,128)(2,1)} %v_ref.1) | copy-start | bytes 393220
  70.2 8.5 %collective-permute-start.1 = (bf16[1024,128]{1,0:T(8,128)(2,1)S(1)}, bf16[1024,128]{1,0:T(8,128)(2,1)S(1)}, u32[]{:S(2)}, u32[]{:S(2)}) collective-permute-start(bf16[1024,128]{1,0:T(8,128)(2,1)S(1)} %get-tuple-element.10), channel_id=1, source_target_pairs={{32,0},{64,32},{96,64},{128,96},{160,128},{192,160},{224,192},{256... | collective-permute-start | bytes 786440 | tf_op jit(solution)/shard_map/ppermute | solution.py:25

commit v3 on v2

--- a/solution.py
+++ b/solution.py
@@ -1,11 +1,10 @@
-import functools
-
 import jax
 import jax.numpy as jnp
 from jax import lax
 from jax.experimental import pallas as pl
 from jax.experimental.pallas import tpu as pltpu
 from jax.sharding import PartitionSpec as P
+
 
 HD = 128
 BLK = 128
@@ -15,6 +14,7 @@
 LIMIT = 24 * 1024 * 1024
 VM = pl.BlockSpec(memory_space=pltpu.VMEM)
 SM = pl.BlockSpec(memory_space=pltpu.SMEM)
+HB = pl.BlockSpec(memory_space=pltpu.HBM)
 F32 = jnp.float32
 BF16 = jnp.bfloat16
 
@@ -37,30 +37,41 @@
     return lax.dot_general(a, b, (((0,), (0,)), ((), ())), preferred_element_type=F32)
 
 
-def call(body, ins, outs, name, flops, nbytes, scratch=()):
+def call(body, ins, outs, flops, nbytes, scratch=(), limit=LIMIT):
     return pl.pallas_call(
         body,
         in_specs=ins,
         out_specs=tuple(VM for _ in outs),
         out_shape=tuple(jax.ShapeDtypeStruct(s, d) for s, d in outs),
         scratch_shapes=list(scratch),
-        compiler_params=pltpu.CompilerParams(vmem_limit_bytes=LIMIT),
+        compiler_params=pltpu.CompilerParams(vmem_limit_bytes=limit),
         cost_estimate=pl.CostEstimate(flops=flops, bytes_accessed=nbytes, transcendentals=0),
-        name=name,
     )
 
 
-def pack_kernel(slot_ref, grad_ref, saved_ref, out_ref, square):
+def pack_kernel(slot_ref, grad_hbm, saved_hbm, out_ref, square, grad_ref, saved_ref, sems):
     heads, rows = out_ref.shape[0], grad_ref.shape[0]
+    half = heads * HD // 2
+    copies = []
+    for i in range(2):
+        part = slice(i * half, (i + 1) * half)
+        for j, (src, dst) in enumerate(((grad_hbm, grad_ref), (saved_hbm, saved_ref))):
+            copy = pltpu.make_async_copy(src.at[:, part], dst.at[:, part], sems.at[i, j])
+            copy.start()
+            copies.append(copy)
+    square[...] = jnp.zeros_like(square)
     lane = lax.broadcasted_iota(jnp.int32, (rows, BLK), 1)
     delta = jnp.zeros((rows, BLK), F32)
     for h in range(heads):
+        if h % (heads // 2) == 0:
+            for copy in copies[:2]:
+                copy.wait()
+            copies = copies[2:]
         g = grad_ref[:, h * HD : (h + 1) * HD]
         for k in range(rows // 2):
             out_ref[h, k] = g[2 * k : 2 * k + 2, :]
         prod = g.astype(F32) * saved_ref[:, h * HD : (h + 1) * HD].astype(F32)
         delta = jnp.where(lane == h, jnp.sum(prod, axis=1, keepdims=True), delta)
-    square[...] = jnp.zeros_like(square)
     start = pl.multiple_of(slot_ref[0] * rows, rows)
     square[pl.ds(start, rows), :] = delta
     turned = square[...].T
@@ -179,22 +190,26 @@
     slot = lax.rem(lax.axis_index("head"), BLK // rows).astype(jnp.int32)[None]
     (packed,) = call(
         pack_kernel,
-        [SM, VM, VM],
+        [SM, HB, HB],
         [((heads, rows // 2 + 1, 2, HD), BF16)],
-        "pack",
         4 * rows * heads * HD,
         6 * rows * heads * HD,
-        [pltpu.VMEM((BLK, BLK), F32)],
+        [
+            pltpu.VMEM((BLK, BLK), F32),
+            pltpu.VMEM(grad_out.shape, BF16),
+            pltpu.VMEM(saved_out.shape, BF16),
+            pltpu.SemaphoreType.DMA((2, 2)),
+        ],
+        60 * 1024 * 1024,
     )(slot, grad_out, saved_out)
+    previous = shifted(jnp.concatenate([key_heads, value_heads], axis=0), "seq", 1)
     arrived = lax.all_to_all(packed, "head", split_axis=0, concat_axis=0, tiled=True)
-    previous = shifted(jnp.concatenate([key_heads, value_heads], axis=0), "seq", 1)
     group_index = lax.axis_index("seq")
     block_rows = lax.dynamic_slice_in_dim(block_list, group_index * qcount, qcount, 0)
     (probs,) = call(
         prob_kernel,
         [SM, VM, VM, VM],
         [((2 * span, span), F32)],
-        "probs",
         4 * span * span * HD,
         12 * span * span,
     )(block_rows, query_heads, key_heads, previous)
@@ -202,7 +217,6 @@
         prev_kernel,
         [VM] * 4,
         [((2 * span, HD), BF16), ((span, HD), F32)],
-        "prev_grads",
         8 * span * span * HD,
         8 * span * span,
     )(probs, arrived, query_heads, previous)
@@ -211,26 +225,15 @@
         own_kernel,
         [VM] * 6,
         [((span, HD), BF16), ((2 * span, HD), F32)],
-        "own_grads",
         8 * span * span * HD,
         8 * span * span,
     )(probs, arrived, query_heads, key_heads, value_heads, dq_part)
     (joined,) = call(
-        join_kernel,
-        [VM] * 3,
-        [((heads, 3 * rows, HD), BF16)],
-        "join",
-        4 * span * HD,
-        16 * span * HD,
+        join_kernel, [VM] * 3, [((heads, 3 * rows, HD), BF16)], 4 * span * HD, 16 * span * HD
     )(grad_query, own, returned)
     landed = lax.all_to_all(joined, "head", split_axis=0, concat_axis=0, tiled=True)
     return call(
-        split_kernel,
-        [VM],
-        [((rows, heads * HD), BF16)] * 3,
-        "split",
-        0,
-        12 * rows * heads * HD,
+        split_kernel, [VM], [((rows, heads * HD), BF16)] * 3, 0, 12 * rows * heads * HD
     )(landed)
 
 

time: 147 us -> 146 us (level)
  local copies, waits for them, and re-layouts: 3.83 us -> 1.99 us
    unnamed x17 -> x13, local copies, waits for them, and re-layouts: 3.75 us -> 1.92 us
where the time goes in v3:
time: 146 us; the launch traced here: 144 us
  blocking collectives  65.8 us (45%)
  starting transfers between devices  35.3 us (24%)
  waiting for transfers between devices  33.8 us (23%)
  Pallas kernels  5.91 us (4%)
  local copies, waits for them, and re-layouts  1.99 us (1%)
    all_to_all x1, blocking collectives, shards(): lax.all_to_all(joined, 'head', split_axis=0, concat_axis=0, tiled=True)  65.8 us
    all_to_all x1, starting transfers between devices, shards(): lax.all_to_all(packed, 'head', split_axis=0, concat_axis=0, tiled=True)  30.7 us
    ppermute x2, waiting for transfers between devices, shifted(): return lax.ppermute(value, axis, pairs)  21.7 us
    all_to_all x1, waiting for transfers between devices, shards(): lax.all_to_all(packed, 'head', split_axis=0, concat_axis=0, tiled=True)  12 us
    ppermute x2, starting transfers between devices, shifted(): return lax.ppermute(value, axis, pairs)  4.57 us
  transfers between devices with their start and end apart: 3, of which 3 were waited for; matrix products, arithmetic and copies ran while one was open for 1% of the time, Pallas kernels for 2%

profile of v3, /device:TPU:57, one launch (start us, length us, event | category | flops | bytes accessed | tf_op | source)
XLA Modules:
  0.0 144.5 jit_solution(5111562774726003123)
XLA Ops:
  0.6 0.0 copy-start
  0.6 0.0 copy-start.2
  0.7 1.9 %shard_map.86 = bf16[32,9,2,128]{3,2,1,0:T(2,128)(2,1)} custom-call(s32[1]{0:T(128)} %bitcast.slot_ref, bf16[16,4096]{1,0:T(8,128)(2,1)} %grad_hbm.1, bf16[16,4096]{1,0:T(8,128)(2,1)} %saved_hbm.1), custom_call_target="tpu_custom_call" | custom-call | flops 262144 | bytes 393216 | tf_op jit(solution)/shard_map/pallas_call | solution.py:191
  2.6 30.7 %all-to-all-start = ((bf16[32,9,2,128]{3,2,1,0:T(2,128)(2,1)}), bf16[32,9,2,128]{3,2,1,0:T(2,128)(2,1)S(1)}, u32[]{:S(2)}, u32[]{:S(2)}) async-start(bf16[32,9,2,128]{3,2,1,0:T(2,128)(2,1)} %shard_map.86), calls=%async_computation | async-start | bytes 294912 | tf_op jit(solution)/shard_map/all_to_all | solution.py:206
  33.3 1.0 pad_maximum_fusion
  34.3 2.6 %collective-permute-start = (bf16[1024,128]{1,0:T(8,128)(2,1)S(1)}, bf16[1024,128]{1,0:T(8,128)(2,1)S(1)}, u32[]{:S(2)}, u32[]{:S(2)}) collective-permute-start(bf16[1024,128]{1,0:T(8,128)(2,1)S(1)} %pad_maximum_fusion), channel_id=1, source_target_pairs={{0,32},{32,64},{64,96},{96,128},{128,160},{160,192},{192,224},{224... | collective-permute-start | bytes 786440 | tf_op jit(solution)/shard_map/ppermute | solution.py:25
  37.0 0.0 copy-done
  37.0 0.1 constant_dynamic-slice_fusion
  37.1 0.1 copy.10.list_ref
  37.2 16.0 %collective-permute-done.prev_ref = bf16[1024,128]{1,0:T(8,128)(2,1)S(1)} collective-permute-done((bf16[1024,128]{1,0:T(8,128)(2,1)S(1)}, bf16[1024,128]{1,0:T(8,128)(2,1)S(1)}, u32[]{:S(2)}, u32[]{:S(2)}) %collective-permute-start) | collective-permute-done | bytes 262176 | tf_op jit(solution)/shard_map/ppermute | solution.py:25
  53.2 0.0 copy-start.1
  53.2 0.9 copy-done.1
  54.1 0.0 copy-start.3
  54.1 0.9 copy-done.3
  55.0 0.0 copy-start.4
  55.0 0.0 copy-start.5
  55.0 1.5 %shard_map.85.p_ref = f32[1024,512]{1,0:T(8,128)S(1)} custom-call(s32[4,8]{1,0:T(4,128)S(1)} %copy.10.list_ref, bf16[512,128]{1,0:T(8,128)(2,1)S(1)} %copy-done.1, bf16[512,128]{1,0:T(8,128)(2,1)S(1)} %copy-done.3, bf16[1024,128]{1,0:T(8,128)(2,1)S(1)} %collective-permute-done.prev_ref), custom_call_target="tpu_custom_call" | custom-call | flops 134217728 | bytes 3145728 | tf_op jit(solution)/shard_map/pallas_call | solution.py:209
  56.5 12.0 %all-to-all-done.recv_ref = bf16[32,9,2,128]{3,2,1,0:T(2,128)(2,1)S(1)} async-done(((bf16[32,9,2,128]{3,2,1,0:T(2,128)(2,1)}), bf16[32,9,2,128]{3,2,1,0:T(2,128)(2,1)S(1)}, u32[]{:S(2)}, u32[]{:S(2)}) %all-to-all-start) | async-done | bytes 147488 | tf_op jit(solution)/shard_map/all_to_all | solution.py:206
  68.5 0.0 copy-done.2
  68.5 0.8 shard_map.87
  69.4 1.9 %collective-permute-start.1 = (bf16[1024,128]{1,0:T(8,128)(2,1)S(1)}, bf16[1024,128]{1,0:T(8,128)(2,1)S(1)}, u32[]{:S(2)}, u32[]{:S(2)}) collective-permute-start(bf16[1024,128]{1,0:T(8,128)(2,1)S(1)} %get-tuple-element.10), channel_id=1, source_target_pairs={{32,0},{64,32},{96,64},{128,96},{160,128},{192,160},{224,192},{256... | collective-permute-start | bytes 786440 | tf_op jit(solution)/shard_map/ppermute | solution.py:25
  71.3 0.0 copy-done.4
  71.3 0.0 copy-done.5
  71.3 0.8 shard_map.88
  72.1 5.7 %collective-permute-done.1.back_ref = bf16[1024,128]{1,0:T(8,128)(2,1)S(1)} collective-permute-done((bf16[1024,128]{1,0:T(8,128)(2,1)S(1)}, bf16[1024,128]{1,0:T(8,128)(2,1)S(1)}, u32[]{:S(2)}, u32[]{:S(2)}) %collective-permute-start.1) | collective-permute-done | bytes 262176 | tf_op jit(solution)/shard_map/ppermute | solution.py:25
  77.8 0.1 shard_map.89
  77.9 65.8 %all_to_all.10.in_ref = bf16[32,48,128]{2,1,0:T(8,128)(2,1)S(1)} all-to-all(bf16[32,48,128]{2,1,0:T(8,128)(2,1)S(1)} %shard_map.89), channel_id=1, replica_groups=mesh['seq'=32,'head'=32] {'head'}, dimensions={0} | all-to-all | bytes 786432 | tf_op jit(solution)/shard_map/all_to_all | solution.py:234
  143.6 0.8 shard_map.90
Async XLA Ops:
  0.6 36.4 %copy-start = (s32[128,8]{0,1:T(8,128)S(1)}, s32[128,8]{0,1:T(8,128)}, u32[]{:S(2)}) copy-start(s32[128,8]{0,1:T(8,128)} %param.11) | copy-start | bytes 12292
  0.6 67.9 %copy-start.2 = (bf16[512,128]{1,0:T(8,128)(2,1)S(1)}, bf16[512,128]{1,0:T(8,128)(2,1)}, u32[]{:S(2)}) copy-start(bf16[512,128]{1,0:T(8,128)(2,1)} %q_ref.5) | copy-start | bytes 393220
  2.6 65.9 %all-to-all-start = ((bf16[32,9,2,128]{3,2,1,0:T(2,128)(2,1)}), bf16[32,9,2,128]{3,2,1,0:T(2,128)(2,1)S(1)}, u32[]{:S(2)}, u32[]{:S(2)}) async-start(bf16[32,9,2,128]{3,2,1,0:T(2,128)(2,1)} %shard_map.86), calls=%async_computation | async-start | bytes 294912 | tf_op jit(solution)/shard_map/all_to_all | solution.py:206
  34.3 18.8 %collective-permute-start = (bf16[1024,128]{1,0:T(8,128)(2,1)S(1)}, bf16[1024,128]{1,0:T(8,128)(2,1)S(1)}, u32[]{:S(2)}, u32[]{:S(2)}) collective-permute-start(bf16[1024,128]{1,0:T(8,128)(2,1)S(1)} %pad_maximum_fusion), channel_id=1, source_target_pairs={{0,32},{32,64},{64,96},{96,128},{128,160},{160,192},{192,224},{224... | collective-permute-start | bytes 786440 | tf_op jit(solution)/shard_map/ppermute | solution.py:25
  53.2 0.9 copy-start.1
  54.1 0.9 copy-start.3
  55.0 16.3 %copy-start.4 = (bf16[512,128]{1,0:T(8,128)(2,1)S(1)}, bf16[512,128]{1,0:T(8,128)(2,1)}, u32[]{:S(2)}) copy-start(bf16[512,128]{1,0:T(8,128)(2,1)} %k_ref.3) | copy-start | bytes 393220
  55.0 16.3 %copy-start.5 = (bf16[512,128]{1,0:T(8,128)(2,1)S(1)}, bf16[512,128]{1,0:T(8,128)(2,1)}, u32[]{:S(2)}) copy-start(bf16[512,128]{1,0:T(8,128)(2,1)} %v_ref.1) | copy-start | bytes 393220
  69.4 8.5 %collective-permute-start.1 = (bf16[1024,128]{1,0:T(8,128)(2,1)S(1)}, bf16[1024,128]{1,0:T(8,128)(2,1)S(1)}, u32[]{:S(2)}, u32[]{:S(2)}) collective-permute-start(bf16[1024,128]{1,0:T(8,128)(2,1)S(1)} %get-tuple-element.10), channel_id=1, source_target_pairs={{32,0},{64,32},{96,64},{128,96},{160,128},{192,160},{224,192},{256... | collective-permute-start | bytes 786440 | tf_op jit(solution)/shard_map/ppermute | solution.py:25

commit v4 on v3

--- a/solution.py
+++ b/solution.py
@@ -25,6 +25,20 @@
     return lax.ppermute(value, axis, pairs)
 
 
+def turned(value, by):
+    size = lax.axis_size("head")
+    pairs = [(h, h - h % 8 + (h + 2 * by) % 8) for h in range(size)]
+    return lax.ppermute(value, "head", pairs)
+
+
+def across(value):
+    size = lax.axis_size("head")
+    groups = [[h for h in range(size) if h % 8 // 2 == z] for z in range(4)]
+    return lax.all_to_all(
+        value, "head", split_axis=0, concat_axis=0, axis_index_groups=groups, tiled=True
+    )
+
+
 def nt(a, b):
     return lax.dot_general(a, b, (((1,), (1,)), ((), ())), preferred_element_type=F32)
 
@@ -49,38 +63,52 @@
     )
 
 
-def pack_kernel(slot_ref, grad_hbm, saved_hbm, out_ref, square, grad_ref, saved_ref, sems):
-    heads, rows = out_ref.shape[0], grad_ref.shape[0]
-    half = heads * HD // 2
+def partner(i, z):
+    return (i // 2) * 8 + lax.rem(z, 4) * 2 + i % 2
+
+
+def pack_kernel(
+    place_ref, grad_hbm, saved_hbm, k_hbm, v_hbm, *refs
+):
+    out_refs, (kv_ref, square, grad_ref, saved_ref, sems) = refs[:4], refs[4:]
+    rows, heads = grad_ref.shape[0], grad_ref.shape[1] // HD
+    span = k_hbm.shape[0]
     copies = []
-    for i in range(2):
-        part = slice(i * half, (i + 1) * half)
-        for j, (src, dst) in enumerate(((grad_hbm, grad_ref), (saved_hbm, saved_ref))):
-            copy = pltpu.make_async_copy(src.at[:, part], dst.at[:, part], sems.at[i, j])
-            copy.start()
-            copies.append(copy)
+    for j, (src, dst) in enumerate(
+        (
+            (grad_hbm, grad_ref),
+            (saved_hbm, saved_ref),
+            (k_hbm, kv_ref.at[0:span]),
+            (v_hbm, kv_ref.at[span : 2 * span]),
+        )
+    ):
+        copy = pltpu.make_async_copy(src, dst, sems.at[j])
+        copy.start()
+        copies.append(copy)
     square[...] = jnp.zeros_like(square)
     lane = lax.broadcasted_iota(jnp.int32, (rows, BLK), 1)
     delta = jnp.zeros((rows, BLK), F32)
-    for h in range(heads):
-        if h % (heads // 2) == 0:
-            for copy in copies[:2]:
-                copy.wait()
-            copies = copies[2:]
-        g = grad_ref[:, h * HD : (h + 1) * HD]
+    copies[0].wait()
+    copies[1].wait()
+    for n in range(heads):
+        j, i = n // 8, n % 8
+        cols = pl.ds(pl.multiple_of(partner(i, place_ref[1] + j) * HD, HD), HD)
+        g = grad_ref[:, cols]
         for k in range(rows // 2):
-            out_ref[h, k] = g[2 * k : 2 * k + 2, :]
-        prod = g.astype(F32) * saved_ref[:, h * HD : (h + 1) * HD].astype(F32)
-        delta = jnp.where(lane == h, jnp.sum(prod, axis=1, keepdims=True), delta)
-    start = pl.multiple_of(slot_ref[0] * rows, rows)
+            out_refs[j][i, k] = g[2 * k : 2 * k + 2, :]
+        prod = g.astype(F32) * saved_ref[:, cols].astype(F32)
+        delta = jnp.where(lane == n, jnp.sum(prod, axis=1, keepdims=True), delta)
+    start = pl.multiple_of(place_ref[0] * rows, rows)
     square[pl.ds(start, rows), :] = delta
     turned = square[...].T
     high = turned.astype(BF16).astype(F32)
     rest = turned - high
     row = lax.broadcasted_iota(jnp.int32, (2, BLK), 0)
-    for h in range(heads):
-        parts = jnp.where(row == 0, high[h : h + 1, :], rest[h : h + 1, :])
-        out_ref[h, rows // 2] = parts.astype(BF16)
+    for n in range(heads):
+        parts = jnp.where(row == 0, high[n : n + 1, :], rest[n : n + 1, :])
+        out_refs[n // 8][n % 8, rows // 2] = parts.astype(BF16)
+    copies[2].wait()
+    copies[3].wait()
 
 
 def prob_kernel(list_ref, q_ref, k_ref, prev_ref, p_ref):
@@ -130,23 +158,20 @@
             p_ref[rows, cols] = jnp.zeros((BLK, 2 * BLK), F32)
 
 
-def received(recv_ref):
-    peers, pairs = recv_ref.shape[0], recv_ref.shape[1] - 1
+def prev_kernel(place_ref, p_ref, recv_ref, q_ref, prev_ref, back_ref, dq_ref, grad_ref, delta_ref):
+    span = q_ref.shape[0]
+    pairs = recv_ref.shape[2] - 1
     rows = 2 * pairs
-    grads = recv_ref[:, 0:pairs].reshape(peers * rows, HD)
-    parts = jnp.sum(recv_ref[:, pairs].astype(F32), axis=1)
-    each = BLK // rows
-    deltas = [
-        jnp.sum(parts[b * each : (b + 1) * each], axis=0, keepdims=True)
-        for b in range(peers // each)
-    ]
-    return grads, deltas
-
-
-def prev_kernel(p_ref, recv_ref, q_ref, prev_ref, back_ref, dq_ref):
-    span = q_ref.shape[0]
-    grads, deltas = received(recv_ref)
-    delta = jnp.concatenate(deltas, axis=1)
+    for i in range(8):
+        for j in range(4):
+            start = pl.multiple_of(partner(i, place_ref[1] + 4 - j) * rows, rows)
+            grad_ref[pl.ds(start, rows), :] = recv_ref[i, j, 0:pairs].reshape(rows, HD)
+    for b in range(span // BLK):
+        parts = recv_ref[2 * b : 2 * b + 2, :, pairs].astype(F32)
+        delta_ref[:, b * BLK : (b + 1) * BLK] = jnp.sum(
+            parts.reshape(16, HD), axis=0, keepdims=True
+        )
+    grads, delta = grad_ref[...], delta_ref[...]
     keys, values = prev_ref[0:span, :], prev_ref[span : 2 * span, :]
     p = p_ref[0:span, :]
     score_grad = (p * (nt(values, grads) - delta)).astype(BF16)
@@ -155,10 +180,9 @@
     dq_ref[...] = tn(score_grad, keys)
 
 
-def own_kernel(p_ref, recv_ref, q_ref, k_ref, v_ref, part_ref, dq_ref, dkv_ref):
+def own_kernel(p_ref, grad_ref, delta_ref, q_ref, k_ref, v_ref, part_ref, dq_ref, dkv_ref):
     span = q_ref.shape[0]
-    grads, deltas = received(recv_ref)
-    delta = jnp.concatenate(deltas, axis=1)
+    grads, delta = grad_ref[...], delta_ref[...]
     p = p_ref[span : 2 * span, :]
     score_grad = (p * (nt(v_ref[...], grads) - delta)).astype(BF16)
     dkv_ref[0:span, :] = nn(score_grad, q_ref[...]) * SCALE
@@ -187,23 +211,27 @@
     qcount = span // BLK
     heads = lax.axis_size("head")
     rows = grad_out.shape[0]
-    slot = lax.rem(lax.axis_index("head"), BLK // rows).astype(jnp.int32)[None]
-    (packed,) = call(
+    at = lax.axis_index("head").astype(jnp.int32)
+    place = jnp.stack([lax.rem(at, 8), lax.rem(at // 2, 4)])
+    slab = (8, rows // 2 + 1, 2, HD)
+    *slabs, both = call(
         pack_kernel,
-        [SM, HB, HB],
-        [((heads, rows // 2 + 1, 2, HD), BF16)],
+        [SM, HB, HB, HB, HB],
+        [(slab, BF16)] * 4 + [((2 * span, HD), BF16)],
         4 * rows * heads * HD,
         6 * rows * heads * HD,
         [
             pltpu.VMEM((BLK, BLK), F32),
             pltpu.VMEM(grad_out.shape, BF16),
             pltpu.VMEM(saved_out.shape, BF16),
-            pltpu.SemaphoreType.DMA((2, 2)),
+            pltpu.SemaphoreType.DMA((4,)),
         ],
         60 * 1024 * 1024,
-    )(slot, grad_out, saved_out)
-    previous = shifted(jnp.concatenate([key_heads, value_heads], axis=0), "seq", 1)
-    arrived = lax.all_to_all(packed, "head", split_axis=0, concat_axis=0, tiled=True)
+    )(place, grad_out, saved_out, key_heads, value_heads)
+    for j in (2, 1, 3):
+        slabs[j] = turned(slabs[j], j)
+    previous = shifted(both, "seq", 1)
+    arrived = across(jnp.stack(slabs, axis=1))
     group_index = lax.axis_index("seq")
     block_rows = lax.dynamic_slice_in_dim(block_list, group_index * qcount, qcount, 0)
     (probs,) = call(
@@ -213,21 +241,21 @@
         4 * span * span * HD,
         12 * span * span,
     )(block_rows, query_heads, key_heads, previous)
-    back, dq_part = call(
+    back, dq_part, grads, delta = call(
         prev_kernel,
-        [VM] * 4,
-        [((2 * span, HD), BF16), ((span, HD), F32)],
+        [SM] + [VM] * 4,
+        [((2 * span, HD), BF16), ((span, HD), F32), ((span, HD), BF16), ((1, span), F32)],
         8 * span * span * HD,
         8 * span * span,
-    )(probs, arrived, query_heads, previous)
+    )(place, probs, arrived, query_heads, previous)
     returned = shifted(back, "seq", -1)
     grad_query, own = call(
         own_kernel,
-        [VM] * 6,
+        [VM] * 7,
         [((span, HD), BF16), ((2 * span, HD), F32)],
         8 * span * span * HD,
         8 * span * span,
-    )(probs, arrived, query_heads, key_heads, value_heads, dq_part)
+    )(probs, grads, delta, query_heads, key_heads, value_heads, dq_part)
     (joined,) = call(
         join_kernel, [VM] * 3, [((heads, 3 * rows, HD), BF16)], 4 * span * HD, 16 * span * HD
     )(grad_query, own, returned)

time: 146 us -> 151 us (1.034)
  the two profiles are of different devices: /device:TPU:57 before, /device:TPU:49 now
where the time goes in v4:
time: 151 us; the launch traced here: 150 us
  blocking collectives  69.9 us (46%)
  starting transfers between devices  57.9 us (38%)
  waiting for transfers between devices  10.1 us (7%)
  Pallas kernels  7.33 us (5%)
  other arithmetic  2.27 us (2%)
  local copies, waits for them, and re-layouts  1.99 us (1%)
    all_to_all x1, blocking collectives, shards(): lax.all_to_all(joined, 'head', split_axis=0, concat_axis=0, tiled=True)  69.9 us
    ppermute x3, starting transfers between devices, turned(): return lax.ppermute(value, 'head', pairs)  41.8 us
    all_to_all x1, starting transfers between devices, across(): lax.all_to_all(value, 'head', split_axis=0, concat_axis=0, axis_index_gro...  8.86 us
    ppermute x2, starting transfers between devices, shifted(): return lax.ppermute(value, axis, pairs)  7.24 us
    ppermute x2, waiting for transfers between devices, shifted(): return lax.ppermute(value, axis, pairs)  5.22 us
    ppermute x3, waiting for transfers between devices, turned(): return lax.ppermute(value, 'head', pairs)  3.04 us
  transfers between devices with their start and end apart: 6, of which 3 were waited for; matrix products, arithmetic and copies ran while one was open for 1% of the time, Pallas kernels for 2%

profile of v4, /device:TPU:49, one launch (start us, length us, event | category | flops | bytes accessed | tf_op | source)
XLA Modules:
  0.0 150.3 jit_solution(10574049603445548632)
XLA Ops:
  0.6 0.0 copy-start
  0.6 0.0 copy-start.2
  0.7 0.6 pad_add_fusion.place_ref
  1.3 0.0 copy-start.6
  1.3 2.8 %shard_map.85 = (bf16[8,9,2,128]{3,2,1,0:T(2,128)(2,1)}, bf16[8,9,2,128]{3,2,1,0:T(2,128)(2,1)}, bf16[8,9,2,128]{3,2,1,0:T(2,128)(2,1)}, bf16[8,9,2,128]{3,2,1,0:T(2,128)(2,1)}, bf16[1024,128]{1,0:T(8,128)(2,1)}) custom-call(s32[2]{0:T(128)} %pad_add_fusion.place_ref, bf16[16,4096]{1,0:T(8,128)(2,1)} %grad_hbm.1, bf16[16,4096]{1,0:T(8,128)(2,1)} %saved_hbm.1, ...), custom_call_target="tpu_custom_call" | custom-call | flops 262144 | bytes 393216 | tf_op jit(solution)/shard_map/pallas_call | solution.py:217
  4.1 15.4 %collective-permute-start.1 = (bf16[8,9,2,128]{3,2,1,0:T(2,128)(2,1)}, bf16[8,9,2,128]{3,2,1,0:T(2,128)(2,1)S(1)}, u32[]{:S(2)}, u32[]{:S(2)}) collective-permute-start(bf16[8,9,2,128]{3,2,1,0:T(2,128)(2,1)} %get-tuple-element.16), channel_id=1, source_target_pairs={{0,2},{1,3},{2,4},{3,5},{4,6},{5,7},{6,0},{7,1},{8,10},{9,11},{10,... | collective-permute-start | bytes 110600 | tf_op jit(solution)/shard_map/ppermute | solution.py:31
  19.5 18.2 %collective-permute-start.2 = (bf16[8,9,2,128]{3,2,1,0:T(2,128)(2,1)}, bf16[8,9,2,128]{3,2,1,0:T(2,128)(2,1)S(1)}, u32[]{:S(2)}, u32[]{:S(2)}) collective-permute-start(bf16[8,9,2,128]{3,2,1,0:T(2,128)(2,1)} %get-tuple-element.17), channel_id=1, source_target_pairs={{0,4},{1,5},{2,6},{3,7},{4,0},{5,1},{6,2},{7,3},{8,12},{9,13},{10,... | collective-permute-start | bytes 110600 | tf_op jit(solution)/shard_map/ppermute | solution.py:31
  37.7 8.2 %collective-permute-start.3 = (bf16[8,9,2,128]{3,2,1,0:T(2,128)(2,1)}, bf16[8,9,2,128]{3,2,1,0:T(2,128)(2,1)S(1)}, u32[]{:S(2)}, u32[]{:S(2)}) collective-permute-start(bf16[8,9,2,128]{3,2,1,0:T(2,128)(2,1)} %get-tuple-element.18), channel_id=1, source_target_pairs={{0,6},{1,7},{2,0},{3,1},{4,2},{5,3},{6,4},{7,5},{8,14},{9,15},{10,... | collective-permute-start | bytes 110600 | tf_op jit(solution)/shard_map/ppermute | solution.py:31
  45.9 2.6 %collective-permute-start = (bf16[1024,128]{1,0:T(8,128)(2,1)}, bf16[1024,128]{1,0:T(8,128)(2,1)S(1)}, u32[]{:S(2)}, u32[]{:S(2)}) collective-permute-start(bf16[1024,128]{1,0:T(8,128)(2,1)} %get-tuple-element.14), channel_id=1, source_target_pairs={{0,32},{32,64},{64,96},{96,128},{128,160},{160,192},{192,224},{224... | collective-permute-start | bytes 786440 | tf_op jit(solution)/shard_map/ppermute | solution.py:25
  48.5 0.0 collective-permute-done.1
  48.5 0.0 collective-permute-done.2
  48.5 3.0 %collective-permute-done.3 = bf16[8,9,2,128]{3,2,1,0:T(2,128)(2,1)S(1)} collective-permute-done((bf16[8,9,2,128]{3,2,1,0:T(2,128)(2,1)}, bf16[8,9,2,128]{3,2,1,0:T(2,128)(2,1)S(1)}, u32[]{:S(2)}, u32[]{:S(2)}) %collective-permute-start.3) | collective-permute-done | bytes 36896 | tf_op jit(solution)/shard_map/ppermute | solution.py:31
  51.6 1.7 %pad_maximum_fusion = bf16[8,4,9,2,128]{4,3,2,1,0:T(2,128)(2,1)} fusion(bf16[8,1,9,2,128]{4,3,2,1,0:T(2,128)(2,1)S(1)} %bitcast.9, bf16[8,1,9,2,128]{4,3,2,1,0:T(2,128)(2,1)S(1)} %bitcast.8, bf16[8,1,9,2,128]{4,3,2,1,0:T(2,128)(2,1)S(1)} %bitcast.7, bf16[8,1,9,2,128]{4,3,2,1,0:T(2,128)(2,1)} %bitcast.6), kind=kLoop, calls=%fused_computation | loop fusion | flops 221184 | bytes 294912 | tf_op jit(solution)/shard_map/stack | solution.py:234
  53.2 8.9 %all-to-all-start = ((bf16[8,4,9,2,128]{4,3,2,1,0:T(2,128)(2,1)}), bf16[8,4,9,2,128]{4,3,2,1,0:T(2,128)(2,1)S(1)}, u32[]{:S(2)}, u32[]{:S(2)}) async-start(bf16[8,4,9,2,128]{4,3,2,1,0:T(2,128)(2,1)} %pad_maximum_fusion), calls=%async_computation | async-start | bytes 294912 | tf_op jit(solution)/shard_map/all_to_all | solution.py:37
  62.1 0.0 copy-done
  62.1 0.1 constant_dynamic-slice_fusion
  62.2 0.1 copy.10.list_ref
  62.3 0.0 collective-permute-done.prev_ref
  62.3 0.0 copy-start.1
  62.3 0.9 copy-done.1
  63.2 0.0 copy-start.3
  63.2 0.9 copy-done.3
  64.1 0.0 copy-start.4
  64.1 0.0 copy-start.5
  64.1 1.6 %shard_map.86.p_ref = f32[1024,512]{1,0:T(8,128)S(1)} custom-call(s32[4,8]{1,0:T(4,128)S(1)} %copy.10.list_ref, bf16[512,128]{1,0:T(8,128)(2,1)S(1)} %copy-done.1, bf16[512,128]{1,0:T(8,128)(2,1)S(1)} %copy-done.3, bf16[1024,128]{1,0:T(8,128)(2,1)S(1)} %collective-permute-done.prev_ref), custom_call_target="tpu_custom_call" | custom-call | flops 134217728 | bytes 3145728 | tf_op jit(solution)/shard_map/pallas_call | solution.py:237
  65.6 1.9 %all-to-all-done.recv_ref = bf16[8,4,9,2,128]{4,3,2,1,0:T(2,128)(2,1)S(1)} async-done(((bf16[8,4,9,2,128]{4,3,2,1,0:T(2,128)(2,1)}), bf16[8,4,9,2,128]{4,3,2,1,0:T(2,128)(2,1)S(1)}, u32[]{:S(2)}, u32[]{:S(2)}) %all-to-all-start) | async-done | bytes 147488 | tf_op jit(solution)/shard_map/all_to_all | solution.py:37
  67.5 0.0 copy-done.2
  67.5 0.0 copy-done.6
  67.5 1.4 shard_map.87
  68.9 4.6 %collective-permute-start.4 = (bf16[1024,128]{1,0:T(8,128)(2,1)S(1)}, bf16[1024,128]{1,0:T(8,128)(2,1)S(1)}, u32[]{:S(2)}, u32[]{:S(2)}) collective-permute-start(bf16[1024,128]{1,0:T(8,128)(2,1)S(1)} %get-tuple-element.24), channel_id=1, source_target_pairs={{32,0},{64,32},{96,64},{128,96},{160,128},{192,160},{224,192},{256... | collective-permute-start | bytes 786440 | tf_op jit(solution)/shard_map/ppermute | solution.py:25
  73.5 0.0 copy-done.4
  73.5 0.0 copy-done.5
  73.5 0.7 shard_map.88
  74.3 5.2 %collective-permute-done.4.back_ref = bf16[1024,128]{1,0:T(8,128)(2,1)S(1)} collective-permute-done((bf16[1024,128]{1,0:T(8,128)(2,1)S(1)}, bf16[1024,128]{1,0:T(8,128)(2,1)S(1)}, u32[]{:S(2)}, u32[]{:S(2)}) %collective-permute-start.4) | collective-permute-done | bytes 262176 | tf_op jit(solution)/shard_map/ppermute | solution.py:25
  79.5 0.1 shard_map.89
  79.6 69.9 %all_to_all.10.in_ref = bf16[32,48,128]{2,1,0:T(8,128)(2,1)S(1)} all-to-all(bf16[32,48,128]{2,1,0:T(8,128)(2,1)S(1)} %shard_map.89), channel_id=1, replica_groups=mesh['seq'=32,'head'=32] {'head'}, dimensions={0} | all-to-all | bytes 786432 | tf_op jit(solution)/shard_map/all_to_all | solution.py:262
  149.4 0.8 shard_map.90
Async XLA Ops:
  0.6 61.5 %copy-start = (s32[128,8]{0,1:T(8,128)S(1)}, s32[128,8]{0,1:T(8,128)}, u32[]{:S(2)}) copy-start(s32[128,8]{0,1:T(8,128)} %param.11) | copy-start | bytes 12292
  0.6 66.8 %copy-start.2 = (bf16[512,128]{1,0:T(8,128)(2,1)S(1)}, bf16[512,128]{1,0:T(8,128)(2,1)}, u32[]{:S(2)}) copy-start(bf16[512,128]{1,0:T(8,128)(2,1)} %q_ref.5) | copy-start | bytes 393220
  1.3 66.2 %copy-start.6 = (s32[2]{0:T(128)S(1)}, s32[2]{0:T(128)}, u32[]{:S(2)}) copy-start(s32[2]{0:T(128)} %pad_add_fusion.place_ref) | copy-start | bytes 28
  4.1 44.5 %collective-permute-start.1 = (bf16[8,9,2,128]{3,2,1,0:T(2,128)(2,1)}, bf16[8,9,2,128]{3,2,1,0:T(2,128)(2,1)S(1)}, u32[]{:S(2)}, u32[]{:S(2)}) collective-permute-start(bf16[8,9,2,128]{3,2,1,0:T(2,128)(2,1)} %get-tuple-element.16), channel_id=1, source_target_pairs={{0,2},{1,3},{2,4},{3,5},{4,6},{5,7},{6,0},{7,1},{8,10},{9,11},{10,... | collective-permute-start | bytes 110600 | tf_op jit(solution)/shard_map/ppermute | solution.py:31
  19.5 29.0 %collective-permute-start.2 = (bf16[8,9,2,128]{3,2,1,0:T(2,128)(2,1)}, bf16[8,9,2,128]{3,2,1,0:T(2,128)(2,1)S(1)}, u32[]{:S(2)}, u32[]{:S(2)}) collective-permute-start(bf16[8,9,2,128]{3,2,1,0:T(2,128)(2,1)} %get-tuple-element.17), channel_id=1, source_target_pairs={{0,4},{1,5},{2,6},{3,7},{4,0},{5,1},{6,2},{7,3},{8,12},{9,13},{10,... | collective-permute-start | bytes 110600 | tf_op jit(solution)/shard_map/ppermute | solution.py:31
  37.7 13.9 %collective-permute-start.3 = (bf16[8,9,2,128]{3,2,1,0:T(2,128)(2,1)}, bf16[8,9,2,128]{3,2,1,0:T(2,128)(2,1)S(1)}, u32[]{:S(2)}, u32[]{:S(2)}) collective-permute-start(bf16[8,9,2,128]{3,2,1,0:T(2,128)(2,1)} %get-tuple-element.18), channel_id=1, source_target_pairs={{0,6},{1,7},{2,0},{3,1},{4,2},{5,3},{6,4},{7,5},{8,14},{9,15},{10,... | collective-permute-start | bytes 110600 | tf_op jit(solution)/shard_map/ppermute | solution.py:31
  45.9 16.4 %collective-permute-start = (bf16[1024,128]{1,0:T(8,128)(2,1)}, bf16[1024,128]{1,0:T(8,128)(2,1)S(1)}, u32[]{:S(2)}, u32[]{:S(2)}) collective-permute-start(bf16[1024,128]{1,0:T(8,128)(2,1)} %get-tuple-element.14), channel_id=1, source_target_pairs={{0,32},{32,64},{64,96},{96,128},{128,160},{160,192},{192,224},{224... | collective-permute-start | bytes 786440 | tf_op jit(solution)/shard_map/ppermute | solution.py:25
  53.2 14.3 %all-to-all-start = ((bf16[8,4,9,2,128]{4,3,2,1,0:T(2,128)(2,1)}), bf16[8,4,9,2,128]{4,3,2,1,0:T(2,128)(2,1)S(1)}, u32[]{:S(2)}, u32[]{:S(2)}) async-start(bf16[8,4,9,2,128]{4,3,2,1,0:T(2,128)(2,1)} %pad_maximum_fusion), calls=%async_computation | async-start | bytes 294912 | tf_op jit(solution)/shard_map/all_to_all | solution.py:37
  62.3 0.9 copy-start.1
  63.2 0.9 copy-start.3
  64.1 9.5 %copy-start.4 = (bf16[512,128]{1,0:T(8,128)(2,1)S(1)}, bf16[512,128]{1,0:T(8,128)(2,1)}, u32[]{:S(2)}) copy-start(bf16[512,128]{1,0:T(8,128)(2,1)} %k_ref.3) | copy-start | bytes 393220
  64.1 9.5 %copy-start.5 = (bf16[512,128]{1,0:T(8,128)(2,1)S(1)}, bf16[512,128]{1,0:T(8,128)(2,1)}, u32[]{:S(2)}) copy-start(bf16[512,128]{1,0:T(8,128)(2,1)} %v_ref.1) | copy-start | bytes 393220
  68.9 10.6 %collective-permute-start.4 = (bf16[1024,128]{1,0:T(8,128)(2,1)S(1)}, bf16[1024,128]{1,0:T(8,128)(2,1)S(1)}, u32[]{:S(2)}, u32[]{:S(2)}) collective-permute-start(bf16[1024,128]{1,0:T(8,128)(2,1)S(1)} %get-tuple-element.24), channel_id=1, source_target_pairs={{32,0},{64,32},{96,64},{128,96},{160,128},{192,160},{224,192},{256... | collective-permute-start | bytes 786440 | tf_op jit(solution)/shard_map/ppermute | solution.py:25

commit v5 on v4

--- a/solution.py
+++ b/solution.py
@@ -61,6 +61,10 @@
         compiler_params=pltpu.CompilerParams(vmem_limit_bytes=limit),
         cost_estimate=pl.CostEstimate(flops=flops, bytes_accessed=nbytes, transcendentals=0),
     )
+
+
+def z_of(place_ref):
+    return lax.rem(place_ref[0] // 2, 4)
 
 
 def partner(i, z):
@@ -92,13 +96,13 @@
     copies[1].wait()
     for n in range(heads):
         j, i = n // 8, n % 8
-        cols = pl.ds(pl.multiple_of(partner(i, place_ref[1] + j) * HD, HD), HD)
+        cols = pl.ds(pl.multiple_of(partner(i, z_of(place_ref) + j) * HD, HD), HD)
         g = grad_ref[:, cols]
         for k in range(rows // 2):
             out_refs[j][i, k] = g[2 * k : 2 * k + 2, :]
         prod = g.astype(F32) * saved_ref[:, cols].astype(F32)
         delta = jnp.where(lane == n, jnp.sum(prod, axis=1, keepdims=True), delta)
-    start = pl.multiple_of(place_ref[0] * rows, rows)
+    start = pl.multiple_of(lax.rem(place_ref[0], 8) * rows, rows)
     square[pl.ds(start, rows), :] = delta
     turned = square[...].T
     high = turned.astype(BF16).astype(F32)
@@ -164,7 +168,7 @@
     rows = 2 * pairs
     for i in range(8):
         for j in range(4):
-            start = pl.multiple_of(partner(i, place_ref[1] + 4 - j) * rows, rows)
+            start = pl.multiple_of(partner(i, z_of(place_ref) + 4 - j) * rows, rows)
             grad_ref[pl.ds(start, rows), :] = recv_ref[i, j, 0:pairs].reshape(rows, HD)
     for b in range(span // BLK):
         parts = recv_ref[2 * b : 2 * b + 2, :, pairs].astype(F32)
@@ -190,6 +194,11 @@
     dq_ref[...] = ((part_ref[...] + tn(score_grad, k_ref[...])) * SCALE).astype(BF16)
 
 
+def stack_kernel(*refs):
+    for j, ref in enumerate(refs[:-1]):
+        refs[-1][:, j] = ref[...]
+
+
 def join_kernel(dq_ref, dkv_ref, back_ref, out_ref):
     peers, rows = out_ref.shape[0], out_ref.shape[1] // 3
     span = dq_ref.shape[0]
@@ -212,7 +221,7 @@
     heads = lax.axis_size("head")
     rows = grad_out.shape[0]
     at = lax.axis_index("head").astype(jnp.int32)
-    place = jnp.stack([lax.rem(at, 8), lax.rem(at // 2, 4)])
+    place = at[None]
     slab = (8, rows // 2 + 1, 2, HD)
     *slabs, both = call(
         pack_kernel,
@@ -231,7 +240,10 @@
     for j in (2, 1, 3):
         slabs[j] = turned(slabs[j], j)
     previous = shifted(both, "seq", 1)
-    arrived = across(jnp.stack(slabs, axis=1))
+    (stacked,) = call(
+        stack_kernel, [VM] * 4, [((8, 4) + slab[1:], BF16)], 0, 4 * rows * heads * HD
+    )(*slabs)
+    arrived = across(stacked)
     group_index = lax.axis_index("seq")
     block_rows = lax.dynamic_slice_in_dim(block_list, group_index * qcount, qcount, 0)
     (probs,) = call(

time: 151 us -> 150 us (level)
  the two profiles are of different devices: /device:TPU:49 before, /device:TPU:57 now
where the time goes in v5:
time: 150 us; the launch traced here: 149 us
  blocking collectives  68.8 us (46%)
  starting transfers between devices  58.8 us (39%)
  waiting for transfers between devices  11.6 us (8%)
  Pallas kernels  6.8 us (5%)
  local copies, waits for them, and re-layouts  2.76 us (2%)
    all_to_all x1, blocking collectives, shards(): lax.all_to_all(joined, 'head', split_axis=0, concat_axis=0, tiled=True)  68.8 us
    ppermute x3, starting transfers between devices, turned(): return lax.ppermute(value, 'head', pairs)  40.9 us
    ppermute x2, starting transfers between devices, shifted(): return lax.ppermute(value, axis, pairs)  9.15 us
    all_to_all x1, starting transfers between devices, across(): lax.all_to_all(value, 'head', split_axis=0, concat_axis=0, axis_index_gro...  8.73 us
    ppermute x3, waiting for transfers between devices, turned(): return lax.ppermute(value, 'head', pairs)  5.7 us
    ppermute x2, waiting for transfers between devices, shifted(): return lax.ppermute(value, axis, pairs)  4.01 us
  transfers between devices with their start and end apart: 6, of which 3 were waited for; matrix products, arithmetic and copies ran while one was open for 0% of the time, Pallas kernels for 2%

profile of v5, /device:TPU:57, one launch (start us, length us, event | category | flops | bytes accessed | tf_op | source)
XLA Modules:
  0.0 149.5 jit_solution(7756276754017318514)
XLA Ops:
  0.6 0.0 copy-start
  0.6 0.0 copy-start.2
  0.7 2.1 %shard_map.85 = (bf16[8,9,2,128]{3,2,1,0:T(2,128)(2,1)}, bf16[8,9,2,128]{3,2,1,0:T(2,128)(2,1)}, bf16[8,9,2,128]{3,2,1,0:T(2,128)(2,1)}, bf16[8,9,2,128]{3,2,1,0:T(2,128)(2,1)}, bf16[1024,128]{1,0:T(8,128)(2,1)}) custom-call(s32[1]{0:T(128)} %bitcast.place_ref, bf16[16,4096]{1,0:T(8,128)(2,1)} %grad_hbm.1, bf16[16,4096]{1,0:T(8,128)(2,1)} %saved_hbm.1, ...), custom_call_target="tpu_custom_call" | custom-call | flops 262144 | bytes 393216 | tf_op jit(solution)/shard_map/pallas_call | solution.py:226
  2.7 3.5 %collective-permute-start = (bf16[1024,128]{1,0:T(8,128)(2,1)}, bf16[1024,128]{1,0:T(8,128)(2,1)S(1)}, u32[]{:S(2)}, u32[]{:S(2)}) collective-permute-start(bf16[1024,128]{1,0:T(8,128)(2,1)} %get-tuple-element.14), channel_id=1, source_target_pairs={{0,32},{32,64},{64,96},{96,128},{128,160},{160,192},{192,224},{224... | collective-permute-start | bytes 786440 | tf_op jit(solution)/shard_map/ppermute | solution.py:25
  6.3 15.4 %collective-permute-start.1 = (bf16[8,9,2,128]{3,2,1,0:T(2,128)(2,1)}, bf16[8,9,2,128]{3,2,1,0:T(2,128)(2,1)S(1)}, u32[]{:S(2)}, u32[]{:S(2)}) collective-permute-start(bf16[8,9,2,128]{3,2,1,0:T(2,128)(2,1)} %get-tuple-element.16), channel_id=1, source_target_pairs={{0,2},{1,3},{2,4},{3,5},{4,6},{5,7},{6,0},{7,1},{8,10},{9,11},{10,... | collective-permute-start | bytes 110600 | tf_op jit(solution)/shard_map/ppermute | solution.py:31
  21.7 17.3 %collective-permute-start.2 = (bf16[8,9,2,128]{3,2,1,0:T(2,128)(2,1)}, bf16[8,9,2,128]{3,2,1,0:T(2,128)(2,1)S(1)}, u32[]{:S(2)}, u32[]{:S(2)}) collective-permute-start(bf16[8,9,2,128]{3,2,1,0:T(2,128)(2,1)} %get-tuple-element.17), channel_id=1, source_target_pairs={{0,4},{1,5},{2,6},{3,7},{4,0},{5,1},{6,2},{7,3},{8,12},{9,13},{10,... | collective-permute-start | bytes 110600 | tf_op jit(solution)/shard_map/ppermute | solution.py:31
  39.0 8.2 %collective-permute-start.3 = (bf16[8,9,2,128]{3,2,1,0:T(2,128)(2,1)}, bf16[8,9,2,128]{3,2,1,0:T(2,128)(2,1)S(1)}, u32[]{:S(2)}, u32[]{:S(2)}) collective-permute-start(bf16[8,9,2,128]{3,2,1,0:T(2,128)(2,1)} %get-tuple-element.18), channel_id=1, source_target_pairs={{0,6},{1,7},{2,0},{3,1},{4,2},{5,3},{6,4},{7,5},{8,14},{9,15},{10,... | collective-permute-start | bytes 110600 | tf_op jit(solution)/shard_map/ppermute | solution.py:31
  47.2 0.0 collective-permute-done.1.refs_1_
  47.2 0.0 collective-permute-done.2.refs_2_
  47.2 5.7 %collective-permute-done.3.refs_3_ = bf16[8,9,2,128]{3,2,1,0:T(2,128)(2,1)S(1)} collective-permute-done((bf16[8,9,2,128]{3,2,1,0:T(2,128)(2,1)}, bf16[8,9,2,128]{3,2,1,0:T(2,128)(2,1)S(1)}, u32[]{:S(2)}, u32[]{:S(2)}) %collective-permute-start.3) | collective-permute-done | bytes 36896 | tf_op jit(solution)/shard_map/ppermute | solution.py:31
  52.9 0.0 copy-start.6
  52.9 0.8 copy-done.6
  53.7 0.7 shard_map.87
  54.4 8.7 %all-to-all-start = ((bf16[8,4,9,2,128]{4,3,2,1,0:T(2,128)(2,1)}), bf16[8,4,9,2,128]{4,3,2,1,0:T(2,128)(2,1)S(1)}, u32[]{:S(2)}, u32[]{:S(2)}) async-start(bf16[8,4,9,2,128]{4,3,2,1,0:T(2,128)(2,1)} %shard_map.87), calls=%async_computation | async-start | bytes 294912 | tf_op jit(solution)/shard_map/all_to_all | solution.py:37
  63.1 0.0 copy-done
  63.1 0.1 constant_dynamic-slice_fusion
  63.2 0.1 copy.10.list_ref
  63.2 0.0 collective-permute-done.prev_ref
  63.3 0.0 copy-start.1
  63.3 0.9 copy-done.1
  64.2 0.0 copy-start.3
  64.2 0.9 copy-done.3
  65.1 0.0 copy-start.4
  65.1 0.0 copy-start.5
  65.1 1.6 %shard_map.86.p_ref = f32[1024,512]{1,0:T(8,128)S(1)} custom-call(s32[4,8]{1,0:T(4,128)S(1)} %copy.10.list_ref, bf16[512,128]{1,0:T(8,128)(2,1)S(1)} %copy-done.1, bf16[512,128]{1,0:T(8,128)(2,1)S(1)} %copy-done.3, bf16[1024,128]{1,0:T(8,128)(2,1)S(1)} %collective-permute-done.prev_ref), custom_call_target="tpu_custom_call" | custom-call | flops 134217728 | bytes 3145728 | tf_op jit(solution)/shard_map/pallas_call | solution.py:249
  66.6 1.8 %all-to-all-done.recv_ref = bf16[8,4,9,2,128]{4,3,2,1,0:T(2,128)(2,1)S(1)} async-done(((bf16[8,4,9,2,128]{4,3,2,1,0:T(2,128)(2,1)}), bf16[8,4,9,2,128]{4,3,2,1,0:T(2,128)(2,1)S(1)}, u32[]{:S(2)}, u32[]{:S(2)}) %all-to-all-start) | async-done | bytes 147488 | tf_op jit(solution)/shard_map/all_to_all | solution.py:37
  68.5 0.0 copy-done.2
  68.5 0.9 shard_map.88
  69.4 5.6 %collective-permute-start.4 = (bf16[1024,128]{1,0:T(8,128)(2,1)S(1)}, bf16[1024,128]{1,0:T(8,128)(2,1)S(1)}, u32[]{:S(2)}, u32[]{:S(2)}) collective-permute-start(bf16[1024,128]{1,0:T(8,128)(2,1)S(1)} %get-tuple-element.24), channel_id=1, source_target_pairs={{32,0},{64,32},{96,64},{128,96},{160,128},{192,160},{224,192},{256... | collective-permute-start | bytes 786440 | tf_op jit(solution)/shard_map/ppermute | solution.py:25
  75.0 0.0 copy-done.4
  75.0 0.0 copy-done.5
  75.0 0.7 shard_map.89
  75.7 4.0 %collective-permute-done.4.back_ref = bf16[1024,128]{1,0:T(8,128)(2,1)S(1)} collective-permute-done((bf16[1024,128]{1,0:T(8,128)(2,1)S(1)}, bf16[1024,128]{1,0:T(8,128)(2,1)S(1)}, u32[]{:S(2)}, u32[]{:S(2)}) %collective-permute-start.4) | collective-permute-done | bytes 262176 | tf_op jit(solution)/shard_map/ppermute | solution.py:25
  79.7 0.1 shard_map.90
  79.8 68.8 %all_to_all.10.in_ref = bf16[32,48,128]{2,1,0:T(8,128)(2,1)S(1)} all-to-all(bf16[32,48,128]{2,1,0:T(8,128)(2,1)S(1)} %shard_map.90), channel_id=1, replica_groups=mesh['seq'=32,'head'=32] {'head'}, dimensions={0} | all-to-all | bytes 786432 | tf_op jit(solution)/shard_map/all_to_all | solution.py:274
  148.7 0.8 shard_map.91
Async XLA Ops:
  0.6 62.5 %copy-start = (s32[128,8]{0,1:T(8,128)S(1)}, s32[128,8]{0,1:T(8,128)}, u32[]{:S(2)}) copy-start(s32[128,8]{0,1:T(8,128)} %param.11) | copy-start | bytes 12292
  0.6 67.8 %copy-start.2 = (bf16[512,128]{1,0:T(8,128)(2,1)S(1)}, bf16[512,128]{1,0:T(8,128)(2,1)}, u32[]{:S(2)}) copy-start(bf16[512,128]{1,0:T(8,128)(2,1)} %q_ref.5) | copy-start | bytes 393220
  2.7 60.5 %collective-permute-start = (bf16[1024,128]{1,0:T(8,128)(2,1)}, bf16[1024,128]{1,0:T(8,128)(2,1)S(1)}, u32[]{:S(2)}, u32[]{:S(2)}) collective-permute-start(bf16[1024,128]{1,0:T(8,128)(2,1)} %get-tuple-element.14), channel_id=1, source_target_pairs={{0,32},{32,64},{64,96},{96,128},{128,160},{160,192},{192,224},{224... | collective-permute-start | bytes 786440 | tf_op jit(solution)/shard_map/ppermute | solution.py:25
  6.3 40.9 %collective-permute-start.1 = (bf16[8,9,2,128]{3,2,1,0:T(2,128)(2,1)}, bf16[8,9,2,128]{3,2,1,0:T(2,128)(2,1)S(1)}, u32[]{:S(2)}, u32[]{:S(2)}) collective-permute-start(bf16[8,9,2,128]{3,2,1,0:T(2,128)(2,1)} %get-tuple-element.16), channel_id=1, source_target_pairs={{0,2},{1,3},{2,4},{3,5},{4,6},{5,7},{6,0},{7,1},{8,10},{9,11},{10,... | collective-permute-start | bytes 110600 | tf_op jit(solution)/shard_map/ppermute | solution.py:31
  21.7 25.5 %collective-permute-start.2 = (bf16[8,9,2,128]{3,2,1,0:T(2,128)(2,1)}, bf16[8,9,2,128]{3,2,1,0:T(2,128)(2,1)S(1)}, u32[]{:S(2)}, u32[]{:S(2)}) collective-permute-start(bf16[8,9,2,128]{3,2,1,0:T(2,128)(2,1)} %get-tuple-element.17), channel_id=1, source_target_pairs={{0,4},{1,5},{2,6},{3,7},{4,0},{5,1},{6,2},{7,3},{8,12},{9,13},{10,... | collective-permute-start | bytes 110600 | tf_op jit(solution)/shard_map/ppermute | solution.py:31
  39.0 13.9 %collective-permute-start.3 = (bf16[8,9,2,128]{3,2,1,0:T(2,128)(2,1)}, bf16[8,9,2,128]{3,2,1,0:T(2,128)(2,1)S(1)}, u32[]{:S(2)}, u32[]{:S(2)}) collective-permute-start(bf16[8,9,2,128]{3,2,1,0:T(2,128)(2,1)} %get-tuple-element.18), channel_id=1, source_target_pairs={{0,6},{1,7},{2,0},{3,1},{4,2},{5,3},{6,4},{7,5},{8,14},{9,15},{10,... | collective-permute-start | bytes 110600 | tf_op jit(solution)/shard_map/ppermute | solution.py:31
  52.9 0.8 copy-start.6
  54.4 14.1 %all-to-all-start = ((bf16[8,4,9,2,128]{4,3,2,1,0:T(2,128)(2,1)}), bf16[8,4,9,2,128]{4,3,2,1,0:T(2,128)(2,1)S(1)}, u32[]{:S(2)}, u32[]{:S(2)}) async-start(bf16[8,4,9,2,128]{4,3,2,1,0:T(2,128)(2,1)} %shard_map.87), calls=%async_computation | async-start | bytes 294912 | tf_op jit(solution)/shard_map/all_to_all | solution.py:37
  63.3 0.9 copy-start.1
  64.2 0.9 copy-start.3
  65.1 9.9 %copy-start.4 = (bf16[512,128]{1,0:T(8,128)(2,1)S(1)}, bf16[512,128]{1,0:T(8,128)(2,1)}, u32[]{:S(2)}) copy-start(bf16[512,128]{1,0:T(8,128)(2,1)} %k_ref.3) | copy-start | bytes 393220
  65.1 9.9 %copy-start.5 = (bf16[512,128]{1,0:T(8,128)(2,1)S(1)}, bf16[512,128]{1,0:T(8,128)(2,1)}, u32[]{:S(2)}) copy-start(bf16[512,128]{1,0:T(8,128)(2,1)} %v_ref.1) | copy-start | bytes 393220
  69.4 10.4 %collective-permute-start.4 = (bf16[1024,128]{1,0:T(8,128)(2,1)S(1)}, bf16[1024,128]{1,0:T(8,128)(2,1)S(1)}, u32[]{:S(2)}, u32[]{:S(2)}) collective-permute-start(bf16[1024,128]{1,0:T(8,128)(2,1)S(1)} %get-tuple-element.24), channel_id=1, source_target_pairs={{32,0},{64,32},{96,64},{128,96},{160,128},{192,160},{224,192},{256... | collective-permute-start | bytes 786440 | tf_op jit(solution)/shard_map/ppermute | solution.py:25

commit v6 on v5

--- a/solution.py
+++ b/solution.py
@@ -71,21 +71,11 @@
     return (i // 2) * 8 + lax.rem(z, 4) * 2 + i % 2
 
 
-def pack_kernel(
-    place_ref, grad_hbm, saved_hbm, k_hbm, v_hbm, *refs
-):
-    out_refs, (kv_ref, square, grad_ref, saved_ref, sems) = refs[:4], refs[4:]
+def pack_kernel(place_ref, grad_hbm, saved_hbm, *refs):
+    out_refs, (square, grad_ref, saved_ref, sems) = refs[:4], refs[4:]
     rows, heads = grad_ref.shape[0], grad_ref.shape[1] // HD
-    span = k_hbm.shape[0]
     copies = []
-    for j, (src, dst) in enumerate(
-        (
-            (grad_hbm, grad_ref),
-            (saved_hbm, saved_ref),
-            (k_hbm, kv_ref.at[0:span]),
-            (v_hbm, kv_ref.at[span : 2 * span]),
-        )
-    ):
+    for j, (src, dst) in enumerate(((grad_hbm, grad_ref), (saved_hbm, saved_ref))):
         copy = pltpu.make_async_copy(src, dst, sems.at[j])
         copy.start()
         copies.append(copy)
@@ -111,8 +101,6 @@
     for n in range(heads):
         parts = jnp.where(row == 0, high[n : n + 1, :], rest[n : n + 1, :])
         out_refs[n // 8][n % 8, rows // 2] = parts.astype(BF16)
-    copies[2].wait()
-    copies[3].wait()
 
 
 def prob_kernel(list_ref, q_ref, k_ref, prev_ref, p_ref):
@@ -162,7 +150,9 @@
             p_ref[rows, cols] = jnp.zeros((BLK, 2 * BLK), F32)
 
 
-def prev_kernel(place_ref, p_ref, recv_ref, q_ref, prev_ref, back_ref, dq_ref, grad_ref, delta_ref):
+def prev_kernel(
+    place_ref, p_ref, recv_ref, q_ref, k_ref, v_ref, back_ref, dq_ref, grad_ref, delta_ref
+):
     span = q_ref.shape[0]
     pairs = recv_ref.shape[2] - 1
     rows = 2 * pairs
@@ -176,7 +166,7 @@
             parts.reshape(16, HD), axis=0, keepdims=True
         )
     grads, delta = grad_ref[...], delta_ref[...]
-    keys, values = prev_ref[0:span, :], prev_ref[span : 2 * span, :]
+    keys, values = k_ref[...], v_ref[...]
     p = p_ref[0:span, :]
     score_grad = (p * (nt(values, grads) - delta)).astype(BF16)
     back_ref[0:span, :] = (nn(score_grad, q_ref[...]) * SCALE).astype(BF16)
@@ -223,23 +213,26 @@
     at = lax.axis_index("head").astype(jnp.int32)
     place = at[None]
     slab = (8, rows // 2 + 1, 2, HD)
-    *slabs, both = call(
-        pack_kernel,
-        [SM, HB, HB, HB, HB],
-        [(slab, BF16)] * 4 + [((2 * span, HD), BF16)],
-        4 * rows * heads * HD,
-        6 * rows * heads * HD,
-        [
-            pltpu.VMEM((BLK, BLK), F32),
-            pltpu.VMEM(grad_out.shape, BF16),
-            pltpu.VMEM(saved_out.shape, BF16),
-            pltpu.SemaphoreType.DMA((4,)),
-        ],
-        60 * 1024 * 1024,
-    )(place, grad_out, saved_out, key_heads, value_heads)
+    slabs = list(
+        call(
+            pack_kernel,
+            [SM, HB, HB],
+            [(slab, BF16)] * 4,
+            4 * rows * heads * HD,
+            6 * rows * heads * HD,
+            [
+                pltpu.VMEM((BLK, BLK), F32),
+                pltpu.VMEM(grad_out.shape, BF16),
+                pltpu.VMEM(saved_out.shape, BF16),
+                pltpu.SemaphoreType.DMA((2,)),
+            ],
+            60 * 1024 * 1024,
+        )(place, grad_out, saved_out)
+    )
     for j in (2, 1, 3):
         slabs[j] = turned(slabs[j], j)
-    previous = shifted(both, "seq", 1)
+    prev_keys = shifted(key_heads, "seq", 1)
+    prev_values = shifted(value_heads, "seq", 1)
     (stacked,) = call(
         stack_kernel, [VM] * 4, [((8, 4) + slab[1:], BF16)], 0, 4 * rows * heads * HD
     )(*slabs)
@@ -252,14 +245,14 @@
         [((2 * span, span), F32)],
         4 * span * span * HD,
         12 * span * span,
-    )(block_rows, query_heads, key_heads, previous)
+    )(block_rows, query_heads, key_heads, prev_keys)
     back, dq_part, grads, delta = call(
         prev_kernel,
-        [SM] + [VM] * 4,
+        [SM] + [VM] * 5,
         [((2 * span, HD), BF16), ((span, HD), F32), ((span, HD), BF16), ((1, span), F32)],
         8 * span * span * HD,
         8 * span * span,
-    )(place, probs, arrived, query_heads, previous)
+    )(place, probs, arrived, query_heads, prev_keys, prev_values)
     returned = shifted(back, "seq", -1)
     grad_query, own = call(
         own_kernel,

time: 150 us -> 149 us (level)
  the two profiles are of different devices: /device:TPU:57 before, /device:TPU:49 now
where the time goes in v6:
time: 149 us; the launch traced here: 148 us
  blocking collectives  69.9 us (47%)
  starting transfers between devices  60.5 us (41%)
  waiting for transfers between devices  7.46 us (5%)
  Pallas kernels  6.63 us (4%)
  local copies, waits for them, and re-layouts  2.76 us (2%)
    all_to_all x1, blocking collectives, shards(): lax.all_to_all(joined, 'head', split_axis=0, concat_axis=0, tiled=True)  69.9 us
    ppermute x3, starting transfers between devices, turned(): return lax.ppermute(value, 'head', pairs)  41.8 us
    ppermute x3, starting transfers between devices, shifted(): return lax.ppermute(value, axis, pairs)  9.89 us
    all_to_all x1, starting transfers between devices, across(): lax.all_to_all(value, 'head', split_axis=0, concat_axis=0, axis_index_gro...  8.86 us
    ppermute x3, waiting for transfers between devices, shifted(): return lax.ppermute(value, axis, pairs)  5.23 us
  transfers between devices with their start and end apart: 7, of which 3 were waited for; matrix products, arithmetic and copies ran while one was open for 0% of the time, Pallas kernels for 2%

profile of v6, /device:TPU:49, one launch (start us, length us, event | category | flops | bytes accessed | tf_op | source)
XLA Modules:
  0.0 148.0 jit_solution(11374764259165841416)
XLA Ops:
  0.6 0.0 copy-start
  0.6 0.0 copy-start.2
  0.7 1.9 %shard_map.86 = (bf16[8,9,2,128]{3,2,1,0:T(2,128)(2,1)}, bf16[8,9,2,128]{3,2,1,0:T(2,128)(2,1)}, bf16[8,9,2,128]{3,2,1,0:T(2,128)(2,1)}, bf16[8,9,2,128]{3,2,1,0:T(2,128)(2,1)}) custom-call(s32[1]{0:T(128)} %bitcast.place_ref, bf16[16,4096]{1,0:T(8,128)(2,1)} %grad_hbm.1, bf16[16,4096]{1,0:T(8,128)(2,1)} %saved_hbm.1), custom_call_target="tpu_custom_call" | custom-call | flops 262144 | bytes 393216 | tf_op jit(solution)/shard_map/pallas_call | solution.py:217
  2.6 15.4 %collective-permute-start.1 = (bf16[8,9,2,128]{3,2,1,0:T(2,128)(2,1)}, bf16[8,9,2,128]{3,2,1,0:T(2,128)(2,1)S(1)}, u32[]{:S(2)}, u32[]{:S(2)}) collective-permute-start(bf16[8,9,2,128]{3,2,1,0:T(2,128)(2,1)} %get-tuple-element.14), channel_id=1, source_target_pairs={{0,2},{1,3},{2,4},{3,5},{4,6},{5,7},{6,0},{7,1},{8,10},{9,11},{10,... | collective-permute-start | bytes 110600 | tf_op jit(solution)/shard_map/ppermute | solution.py:31
  18.0 18.2 %collective-permute-start.2 = (bf16[8,9,2,128]{3,2,1,0:T(2,128)(2,1)}, bf16[8,9,2,128]{3,2,1,0:T(2,128)(2,1)S(1)}, u32[]{:S(2)}, u32[]{:S(2)}) collective-permute-start(bf16[8,9,2,128]{3,2,1,0:T(2,128)(2,1)} %get-tuple-element.15), channel_id=1, source_target_pairs={{0,4},{1,5},{2,6},{3,7},{4,0},{5,1},{6,2},{7,3},{8,12},{9,13},{10,... | collective-permute-start | bytes 110600 | tf_op jit(solution)/shard_map/ppermute | solution.py:31
  36.2 8.2 %collective-permute-start.3 = (bf16[8,9,2,128]{3,2,1,0:T(2,128)(2,1)}, bf16[8,9,2,128]{3,2,1,0:T(2,128)(2,1)S(1)}, u32[]{:S(2)}, u32[]{:S(2)}) collective-permute-start(bf16[8,9,2,128]{3,2,1,0:T(2,128)(2,1)} %get-tuple-element.16), channel_id=1, source_target_pairs={{0,6},{1,7},{2,0},{3,1},{4,2},{5,3},{6,4},{7,5},{8,14},{9,15},{10,... | collective-permute-start | bytes 110600 | tf_op jit(solution)/shard_map/ppermute | solution.py:31
  44.4 2.6 %collective-permute-start = (bf16[512,128]{1,0:T(8,128)(2,1)}, bf16[512,128]{1,0:T(8,128)(2,1)S(1)}, u32[]{:S(2)}, u32[]{:S(2)}) collective-permute-start(bf16[512,128]{1,0:T(8,128)(2,1)} %k_ref.3), channel_id=1, source_target_pairs={{0,32},{32,64},{64,96},{96,128},{128,160},{160,192},{192,224},{224... | collective-permute-start | bytes 393224 | tf_op jit(solution)/shard_map/ppermute | solution.py:25
  47.1 2.6 %collective-permute-start.4 = (bf16[512,128]{1,0:T(8,128)(2,1)}, bf16[512,128]{1,0:T(8,128)(2,1)S(1)}, u32[]{:S(2)}, u32[]{:S(2)}) collective-permute-start(bf16[512,128]{1,0:T(8,128)(2,1)} %v_ref.1), channel_id=1, source_target_pairs={{0,32},{32,64},{64,96},{96,128},{128,160},{160,192},{192,224},{224... | collective-permute-start | bytes 393224 | tf_op jit(solution)/shard_map/ppermute | solution.py:25
  49.7 0.0 collective-permute-done.1.refs_1_
  49.7 0.0 collective-permute-done.2.refs_2_
  49.7 0.4 collective-permute-done.3.refs_3_
  50.1 0.0 copy-start.6
  50.1 0.8 copy-done.6
  50.9 0.7 shard_map.87
  51.6 8.9 %all-to-all-start = ((bf16[8,4,9,2,128]{4,3,2,1,0:T(2,128)(2,1)}), bf16[8,4,9,2,128]{4,3,2,1,0:T(2,128)(2,1)S(1)}, u32[]{:S(2)}, u32[]{:S(2)}) async-start(bf16[8,4,9,2,128]{4,3,2,1,0:T(2,128)(2,1)} %shard_map.87), calls=%async_computation | async-start | bytes 294912 | tf_op jit(solution)/shard_map/all_to_all | solution.py:37
  60.4 0.0 copy-done
  60.4 0.1 constant_dynamic-slice_fusion
  60.5 0.1 copy.10.list_ref
  60.6 0.0 collective-permute-done.prev_ref.k_ref
  60.6 0.0 copy-start.1
  60.6 0.9 copy-done.1
  61.5 0.0 copy-start.3
  61.5 0.9 copy-done.3
  62.4 0.0 copy-start.4
  62.4 0.0 copy-start.5
  62.4 1.5 %shard_map.85.p_ref = f32[1024,512]{1,0:T(8,128)S(1)} custom-call(s32[4,8]{1,0:T(4,128)S(1)} %copy.10.list_ref, bf16[512,128]{1,0:T(8,128)(2,1)S(1)} %copy-done.1, bf16[512,128]{1,0:T(8,128)(2,1)S(1)} %copy-done.3, bf16[512,128]{1,0:T(8,128)(2,1)S(1)} %collective-permute-done.prev_ref.k_ref), custom_call_target="tpu_custom_call" | custom-call | flops 134217728 | bytes 3145728 | tf_op jit(solution)/shard_map/pallas_call | solution.py:242
  64.0 0.0 collective-permute-done.4.v_ref
  64.0 1.9 %all-to-all-done.recv_ref = bf16[8,4,9,2,128]{4,3,2,1,0:T(2,128)(2,1)S(1)} async-done(((bf16[8,4,9,2,128]{4,3,2,1,0:T(2,128)(2,1)}), bf16[8,4,9,2,128]{4,3,2,1,0:T(2,128)(2,1)S(1)}, u32[]{:S(2)}, u32[]{:S(2)}) %all-to-all-start) | async-done | bytes 147488 | tf_op jit(solution)/shard_map/all_to_all | solution.py:37
  65.8 0.0 copy-done.2
  65.8 0.9 shard_map.88
  66.7 4.6 %collective-permute-start.5 = (bf16[1024,128]{1,0:T(8,128)(2,1)S(1)}, bf16[1024,128]{1,0:T(8,128)(2,1)S(1)}, u32[]{:S(2)}, u32[]{:S(2)}) collective-permute-start(bf16[1024,128]{1,0:T(8,128)(2,1)S(1)} %get-tuple-element.22), channel_id=1, source_target_pairs={{32,0},{64,32},{96,64},{128,96},{160,128},{192,160},{224,192},{256... | collective-permute-start | bytes 786440 | tf_op jit(solution)/shard_map/ppermute | solution.py:25
  71.3 0.0 copy-done.4
  71.3 0.0 copy-done.5
  71.3 0.7 shard_map.89
  72.1 5.2 %collective-permute-done.5.back_ref = bf16[1024,128]{1,0:T(8,128)(2,1)S(1)} collective-permute-done((bf16[1024,128]{1,0:T(8,128)(2,1)S(1)}, bf16[1024,128]{1,0:T(8,128)(2,1)S(1)}, u32[]{:S(2)}, u32[]{:S(2)}) %collective-permute-start.5) | collective-permute-done | bytes 262176 | tf_op jit(solution)/shard_map/ppermute | solution.py:25
  77.3 0.1 shard_map.90
  77.4 69.9 %all_to_all.10.in_ref = bf16[32,48,128]{2,1,0:T(8,128)(2,1)S(1)} all-to-all(bf16[32,48,128]{2,1,0:T(8,128)(2,1)S(1)} %shard_map.90), channel_id=1, replica_groups=mesh['seq'=32,'head'=32] {'head'}, dimensions={0} | all-to-all | bytes 786432 | tf_op jit(solution)/shard_map/all_to_all | solution.py:267
  147.2 0.8 shard_map.91
Async XLA Ops:
  0.6 59.8 %copy-start = (s32[128,8]{0,1:T(8,128)S(1)}, s32[128,8]{0,1:T(8,128)}, u32[]{:S(2)}) copy-start(s32[128,8]{0,1:T(8,128)} %param.11) | copy-start | bytes 12292
  0.6 65.2 %copy-start.2 = (bf16[512,128]{1,0:T(8,128)(2,1)S(1)}, bf16[512,128]{1,0:T(8,128)(2,1)}, u32[]{:S(2)}) copy-start(bf16[512,128]{1,0:T(8,128)(2,1)} %q_ref.5) | copy-start | bytes 393220
  2.6 47.1 %collective-permute-start.1 = (bf16[8,9,2,128]{3,2,1,0:T(2,128)(2,1)}, bf16[8,9,2,128]{3,2,1,0:T(2,128)(2,1)S(1)}, u32[]{:S(2)}, u32[]{:S(2)}) collective-permute-start(bf16[8,9,2,128]{3,2,1,0:T(2,128)(2,1)} %get-tuple-element.14), channel_id=1, source_target_pairs={{0,2},{1,3},{2,4},{3,5},{4,6},{5,7},{6,0},{7,1},{8,10},{9,11},{10,... | collective-permute-start | bytes 110600 | tf_op jit(solution)/shard_map/ppermute | solution.py:31
  18.0 31.7 %collective-permute-start.2 = (bf16[8,9,2,128]{3,2,1,0:T(2,128)(2,1)}, bf16[8,9,2,128]{3,2,1,0:T(2,128)(2,1)S(1)}, u32[]{:S(2)}, u32[]{:S(2)}) collective-permute-start(bf16[8,9,2,128]{3,2,1,0:T(2,128)(2,1)} %get-tuple-element.15), channel_id=1, source_target_pairs={{0,4},{1,5},{2,6},{3,7},{4,0},{5,1},{6,2},{7,3},{8,12},{9,13},{10,... | collective-permute-start | bytes 110600 | tf_op jit(solution)/shard_map/ppermute | solution.py:31
  36.2 13.9 %collective-permute-start.3 = (bf16[8,9,2,128]{3,2,1,0:T(2,128)(2,1)}, bf16[8,9,2,128]{3,2,1,0:T(2,128)(2,1)S(1)}, u32[]{:S(2)}, u32[]{:S(2)}) collective-permute-start(bf16[8,9,2,128]{3,2,1,0:T(2,128)(2,1)} %get-tuple-element.16), channel_id=1, source_target_pairs={{0,6},{1,7},{2,0},{3,1},{4,2},{5,3},{6,4},{7,5},{8,14},{9,15},{10,... | collective-permute-start | bytes 110600 | tf_op jit(solution)/shard_map/ppermute | solution.py:31
  44.4 16.2 %collective-permute-start = (bf16[512,128]{1,0:T(8,128)(2,1)}, bf16[512,128]{1,0:T(8,128)(2,1)S(1)}, u32[]{:S(2)}, u32[]{:S(2)}) collective-permute-start(bf16[512,128]{1,0:T(8,128)(2,1)} %k_ref.3), channel_id=1, source_target_pairs={{0,32},{32,64},{64,96},{96,128},{128,160},{160,192},{192,224},{224... | collective-permute-start | bytes 393224 | tf_op jit(solution)/shard_map/ppermute | solution.py:25
  47.1 16.9 %collective-permute-start.4 = (bf16[512,128]{1,0:T(8,128)(2,1)}, bf16[512,128]{1,0:T(8,128)(2,1)S(1)}, u32[]{:S(2)}, u32[]{:S(2)}) collective-permute-start(bf16[512,128]{1,0:T(8,128)(2,1)} %v_ref.1), channel_id=1, source_target_pairs={{0,32},{32,64},{64,96},{96,128},{128,160},{160,192},{192,224},{224... | collective-permute-start | bytes 393224 | tf_op jit(solution)/shard_map/ppermute | solution.py:25
  50.1 0.8 copy-start.6
  51.6 14.3 %all-to-all-start = ((bf16[8,4,9,2,128]{4,3,2,1,0:T(2,128)(2,1)}), bf16[8,4,9,2,128]{4,3,2,1,0:T(2,128)(2,1)S(1)}, u32[]{:S(2)}, u32[]{:S(2)}) async-start(bf16[8,4,9,2,128]{4,3,2,1,0:T(2,128)(2,1)} %shard_map.87), calls=%async_computation | async-start | bytes 294912 | tf_op jit(solution)/shard_map/all_to_all | solution.py:37
  60.6 0.9 copy-start.1
  61.5 0.9 copy-start.3
  62.4 8.9 %copy-start.4 = (bf16[512,128]{1,0:T(8,128)(2,1)S(1)}, bf16[512,128]{1,0:T(8,128)(2,1)}, u32[]{:S(2)}) copy-start(bf16[512,128]{1,0:T(8,128)(2,1)} %k_ref.3) | copy-start | bytes 393220
  62.4 8.9 %copy-start.5 = (bf16[512,128]{1,0:T(8,128)(2,1)S(1)}, bf16[512,128]{1,0:T(8,128)(2,1)}, u32[]{:S(2)}) copy-start(bf16[512,128]{1,0:T(8,128)(2,1)} %v_ref.1) | copy-start | bytes 393220
  66.7 10.6 %collective-permute-start.5 = (bf16[1024,128]{1,0:T(8,128)(2,1)S(1)}, bf16[1024,128]{1,0:T(8,128)(2,1)S(1)}, u32[]{:S(2)}, u32[]{:S(2)}) collective-permute-start(bf16[1024,128]{1,0:T(8,128)(2,1)S(1)} %get-tuple-element.22), channel_id=1, source_target_pairs={{32,0},{64,32},{96,64},{128,96},{160,128},{192,160},{224,192},{256... | collective-permute-start | bytes 786440 | tf_op jit(solution)/shard_map/ppermute | solution.py:25
